TPU v7x, 128 devices: a whole 4x4x4 slice. The times are simulated.
128 devices in a mesh: state: 16 (over y, x_lo, core), plane: 8 (over z, x_hi).
Axes of the slice: x: 4 (x_hi: 2, x_lo: 2; x = x_hi * 2 + x_lo), y: 4, z: 4, core: 2. Of those that a mesh axis runs over, the one named last changes fastest.
Arguments:
- coeffs: float32 [2, 16, 128, 3072], P(None, 'state', None, 'plane'), may hold values from -6 to 6
- mask: int32 [128, 3072], P(None, 'plane'), may hold values 0 or 1
- stick_cols: int32 [3072], replicated, may hold values from 0 to 8191, as said below
- core: float32 [128, 64, 128], P('plane'), may hold values from 0.05 to 0.5
Outputs:
- forces: float32 [2, 16, 128, 3072], P(None, 'state', None, 'plane')
Inputs may be any that keep to these rules, and one draw needn't show every extreme that they name: `stick_cols`: distinct values; 0 and 8191 are always among them.
All inputs are finite; a program needn't handle non-finite values. No bound on the sum of `mask` on one device may be relied on, other than what follows from the above.
Results may differ from a plain program's by a relative error of at most 0.0003.
Values sent between devices are 32-bit elements; how exact they have to be, the bound alone decides.
A program may use at most 128 MiB of HBM per device.

v0:
```python
import math

import jax
import jax.numpy as jnp
from jax import lax
from jax.sharding import PartitionSpec as P

NZ = 128
NX = 64
NY = 128
NSTICK = 3072


spacing = 0.5
pbe_kappa = 0.804
pbe_mu = 0.2195
highest = lax.Precision.HIGHEST


def xc_energy(density, grad_sq):
    exch_const = 0.75 * (3.0 / math.pi) ** (1.0 / 3.0)
    scaled = grad_sq / (4.0 * (3.0 * math.pi**2) ** (2.0 / 3.0) * density ** (8.0 / 3.0))
    enhance = 1.0 + pbe_kappa - pbe_kappa / (1.0 + pbe_mu * scaled / pbe_kappa)
    exchange = -exch_const * density ** (4.0 / 3.0) * enhance
    radius = (3.0 / (4.0 * math.pi * density)) ** (1.0 / 3.0)
    correlation = -0.44 * density / (7.8 + radius)
    return exchange + correlation


def tables(positions, count):
    freqs = jnp.arange(count, dtype=jnp.int32)
    phase = positions[:, None] * freqs[None, :] % count
    angle = phase.astype(jnp.float32) * (2.0 * math.pi / count)
    return (jnp.cos(angle), jnp.sin(angle))


def rotate(real_part, imag_part, cosines, sines, sign, form):

    def apply(values, table):
        return jnp.einsum(form, values, table, precision=highest)

    if imag_part is None:
        return (apply(real_part, cosines), sign * apply(real_part, sines))
    new_real = apply(real_part, cosines) - sign * apply(imag_part, sines)
    new_imag = apply(imag_part, cosines) + sign * apply(real_part, sines)
    return (new_real, new_imag)


def rotate_real(real_part, imag_part, cosines, sines, sign, form):
    first = jnp.einsum(form, real_part, cosines, precision=highest)
    return first - sign * jnp.einsum(form, imag_part, sines, precision=highest)


def signed_freq(index, count):
    signed = jnp.where(index >= count // 2, index - count, index)
    deriv = jnp.where(index == count // 2, 0, signed)
    return (signed.astype(jnp.float32), deriv.astype(jnp.float32))


def on_device(coeffs, mask, stick_cols, core):
    planes_dev = core.shape[0]
    batch = coeffs.shape[1]
    states_all = batch * lax.axis_size("state")
    cells = NX * NY * NZ
    norm = 1.0 / math.sqrt(4.0 * NSTICK * NZ)
    zcos, zsin = tables(jnp.arange(NZ, dtype=jnp.int32), NZ)
    xcos, xsin = tables(jnp.arange(NX, dtype=jnp.int32), NX)
    ycos, ysin = tables(jnp.arange(NY, dtype=jnp.int32), NY)
    mask_f = mask.astype(jnp.float32)
    masked = coeffs * mask_f
    column_real, column_imag = rotate(masked[0], masked[1], zcos, zsin, 1.0, "bgt,gz->bzt")
    columns = jnp.stack([column_real, column_imag])
    sent = lax.all_to_all(columns, "plane", split_axis=2, concat_axis=3, tiled=True)
    count = sent.shape[1]
    empty = jnp.zeros((2, count, planes_dev, NX * NY), jnp.float32)
    placed = empty.at[:, :, :, stick_cols].set(sent).reshape(2, count, planes_dev, NX, NY)
    yreal, yimag = rotate(placed[0], placed[1], ycos, ysin, 1.0, "bzxg,gy->bzxy")
    wreal, wimag = rotate(yreal, yimag, xcos, xsin, 1.0, "bzgy,gx->bzxy")
    pieces = [(wreal * norm, wimag * norm)]
    wave_real = jnp.concatenate([piece[0] for piece in pieces], axis=0)
    wave_imag = jnp.concatenate([piece[1] for piece in pieces], axis=0)
    partial_value = jnp.sum(wave_real * wave_real + wave_imag * wave_imag, axis=0) / states_all
    position = jnp.arange(NZ, dtype=jnp.int32)
    groups = lax.axis_size("state") * lax.axis_size("plane")
    local_planes = planes_dev // lax.axis_size("state")
    block = lax.axis_index("state") * lax.axis_size("plane") + lax.axis_index("plane")
    owner = position // local_planes
    zpos = (
        owner % lax.axis_size("plane") * planes_dev
        + owner // lax.axis_size("plane") * local_planes
        + position % local_planes
    )
    summed = lax.psum_scatter(partial_value, "state", scatter_dimension=0, tiled=True)
    density = summed + lax.dynamic_slice_in_dim(
        core, lax.axis_index("state") * local_planes, local_planes, 0
    )
    pcos, psin = tables(zpos, NZ)
    width_q = NX * NY // groups
    local_planes = density.shape[0]

    def grid_forward(fields):
        count = fields.shape[0]
        areal, aimag = rotate(fields, None, xcos, xsin, -1.0, "mzxy,xg->mzgy")
        breal, bimag = rotate(areal, aimag, ycos, ysin, -1.0, "mzgy,yh->mzgh")
        flat = jnp.stack([breal, bimag]).reshape(2, count, local_planes, NX * NY)
        turned = lax.all_to_all(flat, ("state", "plane"), split_axis=3, concat_axis=2, tiled=True)
        return rotate(turned[0], turned[1], pcos, psin, -1.0, "mpq,pk->mkq")

    def grid_inverse(real_part, imag_part):
        count = real_part.shape[0]
        preal, pimag = rotate(real_part, imag_part, pcos, psin, 1.0, "mkq,pk->mpq")
        flat = jnp.stack([preal, pimag])
        back = lax.all_to_all(flat, ("state", "plane"), split_axis=2, concat_axis=3, tiled=True)
        back = back.reshape(2, count, local_planes, NX, NY)
        areal, aimag = rotate(back[0], back[1], ycos, ysin, 1.0, "mzgh,hy->mzgy")
        return rotate_real(areal, aimag, xcos, xsin, 1.0, "mzgy,gx->mzxy") / cells

    flat_index = block * width_q + jnp.arange(width_q, dtype=jnp.int32)
    sz, dz = signed_freq(position, NZ)
    sx, dx = signed_freq(flat_index // NY, NX)
    sy, dy = signed_freq(flat_index % NY, NY)
    fz = 2.0 * math.pi / (NZ * spacing)
    fx = 2.0 * math.pi / (NX * spacing)
    fy = 2.0 * math.pi / (NY * spacing)
    deriv_z = (dz * fz)[:, None]
    deriv_x = (dx * fx)[None, :]
    deriv_y = (dy * fy)[None, :]
    g_sq = (sz * fz)[:, None] ** 2 + (sx * fx)[None, :] ** 2 + (sy * fy)[None, :] ** 2
    hart = jnp.where(g_sq > 0, 4.0 * math.pi / jnp.where(g_sq > 0, g_sq, 1.0), 0.0)
    rho_real, rho_imag = grid_forward(density[None])
    grad_real = jnp.stack([-deriv_z * rho_imag[0], -deriv_x * rho_imag[0], -deriv_y * rho_imag[0]])
    grad_imag = jnp.stack([deriv_z * rho_real[0], deriv_x * rho_real[0], deriv_y * rho_real[0]])
    grads = grid_inverse(grad_real, grad_imag)
    grad_sq = grads[0] * grads[0] + grads[1] * grads[1] + grads[2] * grads[2]
    unused, pullback = jax.vjp(xc_energy, density, grad_sq)
    v_local, de_dg = pullback(jnp.ones_like(density))
    fluxes = 2.0 * de_dg[None] * grads
    flux_real, flux_imag = grid_forward(fluxes)
    comb_real = (
        hart * rho_real[0]
        + deriv_z * flux_imag[0]
        + deriv_x * flux_imag[1]
        + deriv_y * flux_imag[2]
    )
    comb_imag = (
        hart * rho_imag[0]
        - deriv_z * flux_real[0]
        - deriv_x * flux_real[1]
        - deriv_y * flux_real[2]
    )
    potential = v_local + grid_inverse(comb_real[None], comb_imag[None])[0]
    potential = lax.all_gather(potential, "state", axis=0, tiled=True)
    count = wave_real.shape[0]
    areal, aimag = rotate(
        potential * wave_real, potential * wave_imag, xcos, xsin, -1.0, "bzxy,xg->bzgy"
    )
    breal, bimag = rotate(areal, aimag, ycos, ysin, -1.0, "bzgy,yh->bzgh")
    flat = jnp.stack([breal, bimag]).reshape(2, count, planes_dev, NX * NY)
    picked = jnp.take(flat, stick_cols, axis=3)
    returned = lax.all_to_all(picked, "plane", split_axis=3, concat_axis=2, tiled=True)
    back = returned
    force_real, force_imag = rotate(back[0], back[1], zcos, zsin, -1.0, "bzt,zg->bgt")
    factor = -mask_f / (cells * norm)
    return jnp.stack([force_real * factor, force_imag * factor])


def solution(mesh):
    in_specs = (P(None, "state", None, "plane"), P(None, "plane"), P(), P("plane", None, None))
    out_specs = P(None, "state", None, "plane")
    return jax.shard_map(
        on_device, mesh=mesh, in_specs=in_specs, out_specs=out_specs, check_vma=False
    )
```

profile of v0, /device:TPU:1, one launch (start us, length us, event | category | flops | bytes accessed | tf_op | source)
XLA Modules:
  0.0 899.6 jit_solution(10333308321979161109)
XLA Ops:
  6.5 1.0 convert_element_type.194
  7.5 1.0 broadcast_multiply_fusion
  11.0 1.2 copy.86
  12.2 8.3 all-to-all-start
  21.7 8.1 all-to-all-done
  30.0 1.7 copy.87
  31.7 5.4 broadcast.670
  37.2 280.2 %scatter_fusion = f32[2,16,8192]{1,0,2:T(2,128)} fusion(f32[2,16,8192]{1,0,2:T(2,128)} %broadcast.670, s32[3072]{0:T(1024)S(1)} %get-tuple-element.24, f32[3072,2,16]{2,1,0:T(2,128)S(1)} %bitcast.333), kind=kCustom, calls=%fused_computation.1 | custom fusion | bytes 1191936 | tf_op jit(solution)/shard_map/scatter | solution.py:76
  317.3 11.6 %fusion.475 = (f32[1,16,8192]{1,0,2:T(1,128)}, f32[1,16,8192]{1,0,2:T(1,128)}) fusion(f32[2,16,8192]{1,0,2:T(2,128)} %scatter_fusion), kind=kLoop, calls=%fused_computation.523 | loop fusion | bytes 2097152 | tf_op jit(solution)/shard_map/slice | solution.py:77
  328.9 2.9 copy.108
  332.6 2.9 copy.109
  340.8 0.9 multiply_bitcast_fusion
  341.8 56.5 %reduce-scatter.2.cloned.1.call-done = f32[1,64,128]{2,1,0:T(8,128)} async-done(((f32[16,64,128]{2,1,0:T(8,128)}), f32[1,64,128]{2,1,0:T(8,128)}) %reduce-scatter.2.cloned.1.call-update) | async-done | bytes 32784 | tf_op jit(solution)/shard_map/reduce_scatter | solution.py:93
  401.0 6.4 copy.90
  407.9 6.4 copy.91
  414.3 11.5 %fusion.478 = f32[8192,1,1,2]{3,2,1,0:T(1,128)} fusion(f32[1,1,1,8192]{0,2,1,3:T(1,128)} %copy.91, f32[1,1,1,8192]{0,2,1,3:T(1,128)} %copy.90), kind=kLoop, calls=%fused_computation.526 | loop fusion | flops 16384 | bytes 131072
  426.4 38.5 %reduce.12 = f32[8192,2]{1,0:T(8,128)} reduce(f32[8192,1,1,2]{3,2,1,0:T(1,128)} %fusion.478, f32[]{:T(128)} %broadcast.1063), dimensions={1,2}, to_apply=%fusion.478.reduce_sub_computation | reduce | bytes 131076
  464.8 5.2 reshape.742
  470.0 10.3 %all-to-all-start.1 = ((f32[128,1,128]{2,1,0:T(1,128)}), f32[128,1,128]{2,1,0:T(1,128)S(1)}, u32[]{:S(2)}, u32[]{:S(2)}) async-start(f32[128,1,128]{2,1,0:T(1,128)} %reshape.742), calls=%async_computation.2 | async-start | bytes 131072 | tf_op jit(solution)/shard_map/all_to_all | solution.py:106
  480.3 9.8 %all-to-all-done.1 = f32[128,1,128]{2,1,0:T(1,128)S(1)} async-done(((f32[128,1,128]{2,1,0:T(1,128)}), f32[128,1,128]{2,1,0:T(1,128)S(1)}, u32[]{:S(2)}, u32[]{:S(2)}) %all-to-all-start.1) | async-done | bytes 65568 | tf_op jit(solution)/shard_map/all_to_all | solution.py:106
  491.0 8.1 reshape.743
  499.1 135.9 %slice_reduce_fusion.1 = (f32[8192]{0:T(1024)S(1)}, f32[8192]{0:T(1024)S(1)}) fusion(f32[2,1,1,8192]{0,2,1,3:T(1,128)} %bitcast.324), kind=kLoop, calls=%fused_computation.3 | loop fusion | bytes 131072 | tf_op jit(solution)/shard_map/slice | solution.py:107
  640.4 14.5 %all_to_all.69 = f32[128,1,384]{2,1,0:T(1,128)S(1)} all-to-all(f32[128,1,384]{2,1,0:T(1,128)S(1)} %reshape.744), channel_id=1, replica_groups=mesh['state'=16,'plane'=8] {'state','plane'}, dimensions={0} | all-to-all | bytes 393216 | tf_op jit(solution)/shard_map/all_to_all | solution.py:113
  655.0 1.1 reduce.14
  662.7 12.5 %copy.95 = f32[2,3,1,8192]{1,2,0,3:T(1,128)} copy(f32[2,3,1,8192]{3,1,2,0:T(4,128)S(1)} %pad_maximum_fusion.4) | data formatting | bytes 393216 | tf_op jit(solution)/shard_map/stack | solution.py:105
  675.2 30.8 %reduce.15 = f32[8192,2,3]{2,1,0:T(2,128)} reduce(f32[8192,2,1,3]{3,2,1,0:T(1,128)} %bitcast.325, f32[]{:T(128)} %broadcast.1063), dimensions={2}, to_apply=%bitcast.260.reduce_sub_computation | reduce | bytes 393220
  706.0 14.2 %reshape.746 = f32[128,1,384]{2,1,0:T(1,128)} reshape(f32[8192,2,3]{2,1,0:T(2,128)} %reduce.15) | data formatting | bytes 393216
  720.2 4.7 all-to-all-start.3
  724.9 10.4 %all-to-all-done.3 = f32[128,1,384]{2,1,0:T(1,128)S(1)} async-done(((f32[128,1,384]{2,1,0:T(1,128)}), f32[128,1,384]{2,1,0:T(1,128)S(1)}, u32[]{:S(2)}, u32[]{:S(2)}) %all-to-all-start.3) | async-done | bytes 196640 | tf_op jit(solution)/shard_map/all_to_all | solution.py:106
  735.4 1.1 reduce.16
  736.5 13.5 %reshape.747 = f32[8192,2,1,3]{3,2,1,0:T(1,128)} reshape(f32[128,384]{1,0:T(8,128)S(1)} %reduce.16) | data formatting | bytes 393216
  750.0 7.2 fusion.474
  757.3 3.7 copy.99
  762.2 3.8 copy.97
  769.6 1.1 reduce.17
  771.4 4.5 all-to-all-start.4
  775.9 9.8 %all-to-all-done.4 = f32[128,1,128]{2,1,0:T(1,128)S(1)} async-done(((f32[128,1,128]{2,1,0:T(1,128)}), f32[128,1,128]{2,1,0:T(1,128)S(1)}, u32[]{:S(2)}, u32[]{:S(2)}) %all-to-all-start.4) | async-done | bytes 65568 | tf_op jit(solution)/shard_map/all_to_all | solution.py:113
  785.8 0.8 reduce.18
  789.7 19.3 %all_gather.3 = f32[16,64,128]{2,1,0:T(8,128)S(1)} all-gather(f32[1,64,128]{2,1,0:T(8,128)S(1)} %fusion.31), channel_id=1, replica_groups=mesh['state'=16,'plane'=8] {'state'}, dimensions={0}, use_global_device_ids=true | all-gather | bytes 557056 | tf_op jit(solution)/shard_map/all_gather | solution.py:152
  815.5 8.0 copy.103
  823.6 24.7 %gather_fusion = f32[3072,2,16]{2,1,0:T(2,128)} fusion(f32[2,16,8192]{1,0,2:T(2,128)} %bitcast.332, s32[3072]{0:T(1024)S(1)} %copy-done.3), kind=kCustom, calls=%fused_computation | custom fusion | bytes 798720 | tf_op jit(solution)/shard_map/jit(_take)/gather | solution.py:159
  848.3 12.0 %fusion.479 = f32[3072,1,2,16]{3,2,1,0:T(2,128)S(1)} fusion(f32[3072,2,16]{2,1,0:T(2,128)} %gather_fusion, pred[3072]{0:T(1024)(128)(4,1)S(1)} %compare_and_fusion), kind=kLoop, calls=%fused_computation.527 | loop fusion | flops 98304 | bytes 789504
  860.3 4.1 reshape.750
  864.5 13.8 %all_to_all.70 = f32[8,1,12288]{2,1,0:T(1,128)S(1)} all-to-all(f32[8,1,12288]{2,1,0:T(1,128)S(1)} %reshape.750), channel_id=1, replica_groups=mesh['state'=16,'plane'=8] {'plane'}, dimensions={0} | all-to-all | bytes 786432 | tf_op jit(solution)/shard_map/all_to_all | solution.py:160
  878.3 2.5 reduce.19
  880.8 5.3 reshape.751
  886.1 2.1 copy.116
  888.1 1.0 fusion.476
  (125 shorter events, 44.6 us)
Async XLA Ops:
  6.5 14.5 %copy-start.1 = (s32[3072]{0:T(1024)S(1)}, s32[3072]{0:T(1024)}, u32[]{:S(2)}) copy-start(s32[3072]{0:T(1024)} %param.6) | copy-start | bytes 36868
  12.2 17.6 %all-to-all-start = ((f32[2,1,128,384]{3,1,0,2:T(1,128)}), f32[2,1,128,384]{3,1,0,2:T(1,128)S(1)}, u32[]{:S(2)}, u32[]{:S(2)}) async-start(f32[2,1,128,384]{3,1,0,2:T(1,128)} %copy.86), calls=%async_computation | async-start | bytes 786432 | tf_op jit(solution)/shard_map/all_to_all | solution.py:73
  20.5 377.9 %reduce-scatter.2.cloned.1.call-start = ((), (), s32[]{:S(2)}) async-start(), calls=%async_computation.7 | async-start | bytes 557056 | tf_op jit(solution)/shard_map/reduce_scatter | solution.py:93
  470.0 20.1 %all-to-all-start.1 = ((f32[128,1,128]{2,1,0:T(1,128)}), f32[128,1,128]{2,1,0:T(1,128)S(1)}, u32[]{:S(2)}, u32[]{:S(2)}) async-start(f32[128,1,128]{2,1,0:T(1,128)} %reshape.742), calls=%async_computation.2 | async-start | bytes 131072 | tf_op jit(solution)/shard_map/all_to_all | solution.py:106
  720.2 15.2 %all-to-all-start.3 = ((f32[128,1,384]{2,1,0:T(1,128)}), f32[128,1,384]{2,1,0:T(1,128)S(1)}, u32[]{:S(2)}, u32[]{:S(2)}) async-start(f32[128,1,384]{2,1,0:T(1,128)} %reshape.746), calls=%async_computation.4 | async-start | bytes 393216 | tf_op jit(solution)/shard_map/all_to_all | solution.py:106
  761.0 14.9 %copy-start.2 = (s32[3072]{0:T(1024)S(1)}, s32[3072]{0:T(1024)}, u32[]{:S(2)}) copy-start(s32[3072]{0:T(1024)} %param.6) | copy-start | bytes 36868
  771.4 14.3 %all-to-all-start.4 = ((f32[128,1,128]{2,1,0:T(1,128)}), f32[128,1,128]{2,1,0:T(1,128)S(1)}, u32[]{:S(2)}, u32[]{:S(2)}) async-start(f32[128,1,128]{2,1,0:T(1,128)} %reshape.748), calls=%async_computation.5 | async-start | bytes 131072 | tf_op jit(solution)/shard_map/all_to_all | solution.py:113
  815.5 8.0 copy-start.3
  880.8 9.8 %copy-start = (s32[128,384]{1,0:T(8,128)S(1)}, s32[128,384]{1,0:T(8,128)}, u32[]{:S(2)}) copy-start(s32[128,384]{1,0:T(8,128)} %param.5) | copy-start | bytes 589828
Sparse Core Ops, SparseCore 0:
  341.8 56.4 reduce-scatter.1
where the time goes:
time: 907 us; the launch traced here: 900 us
  local copies, waits for them, and re-layouts  572 us (63%)
  other arithmetic  106 us (12%)
  waiting for transfers between devices  94.8 us (10%)
  blocking collectives  47.6 us (5%)
  matrix products  36 us (4%)
  starting transfers between devices  28.3 us (3%)
  between operations  14.6 us (2%)
    scatter x1, local copies, waits for them, and re-layouts, on_device(): empty.at[:, :, :, stick_cols].set(sent)  280 us
    slice x2, local copies, waits for them, and re-layouts, grid_forward(): return rotate(turned[0], turned[1], pcos, psin, -1.0, 'mpq,pk->mkq')  143 us
    unnamed x5, other arithmetic  93.9 us
    reduce_scatter x1, waiting for transfers between devices, on_device(): lax.psum_scatter(partial_value, 'state', scatter_dimension=0, tiled=True)  56.5 us
    unnamed x20, local copies, waits for them, and re-layouts  52.9 us
    dot_general x52, matrix products, apply(): return jnp.einsum(form, values, table, precision=highest)  30.1 us
    another operation x5, local copies, waits for them, and re-layouts, grid_forward(): flat = jnp.stack([breal, bimag]).reshape(2, count, local_planes, NX * NY)  25.4 us
    gather x1, local copies, waits for them, and re-layouts, on_device(): picked = jnp.take(flat, stick_cols, axis=3)  24.7 us
  transfers between devices with their start and end apart: 5, of which 5 were waited for; matrix products, arithmetic and copies ran while one was open for 0% of the time, Pallas kernels for 0%

commit v1 on v0

v1 whole, which is shorter than its diff:
```python
import functools
import math

import jax
import jax.numpy as jnp
import ml_dtypes
import numpy as np
from jax import lax
from jax.experimental import pallas as pl
from jax.experimental.pallas import tpu as pltpu
from jax.sharding import PartitionSpec as P

NZ = 128
NX = 64
NY = 128
NSTICK = 3072
STATES = 16
PLANES = 8
CHUNK = NSTICK // PLANES
SPACING = 0.5
CELLS = NX * NY * NZ
NORM = 1.0 / math.sqrt(4.0 * NSTICK * NZ)
F32 = jnp.float32
BF16 = jnp.bfloat16
MESH = pl.DeviceIdType.MESH
VMEM_LIMIT = 60 * 1024 * 1024


def two_parts(table):
    high = np.asarray(table, np.float64).astype(ml_dtypes.bfloat16)
    low = (np.asarray(table, np.float64) - high.astype(np.float64)).astype(ml_dtypes.bfloat16)
    return np.stack([high, low])


def wave_table(out_freq, in_freq, count, sign):
    angle = 2.0 * np.pi * (np.outer(out_freq, in_freq) % count) / count
    cos, sin = np.cos(angle), sign * np.sin(angle)
    return np.block([[cos, -sin], [sin, cos]])


def derivative_matrix(count):
    signed = np.arange(count)
    signed = np.where(signed >= count // 2, signed - count, signed)
    deriv = np.where(signed == -(count // 2), 0, signed) * 2.0 * np.pi / (count * SPACING)
    return np.real(np.fft.ifft(1j * deriv[:, None] * np.fft.fft(np.eye(count), axis=0), axis=0))


def cas_matrix(count):
    angle = 2.0 * np.pi * (np.outer(np.arange(count), np.arange(count)) % count) / count
    return np.cos(angle) + np.sin(angle)


def squared_freq(count):
    signed = np.arange(count)
    signed = np.where(signed >= count // 2, signed - count, signed)
    return (signed * 2.0 * np.pi / (count * SPACING)) ** 2


@functools.cache
def tables():
    steps = np.arange(128)
    zwave = wave_table(steps, steps, NZ, 1.0).reshape(2, PLANES, 16, 256)
    zin = NORM * zwave.transpose(1, 0, 2, 3).reshape(256, 256)
    zwave = wave_table(steps, steps, NZ, -1.0).reshape(256, 2, PLANES, 16)
    zout = -zwave.transpose(0, 2, 1, 3).reshape(256, 256) / (CELLS * NORM)
    yin = wave_table(steps, steps, NY, 1.0).T
    yout = wave_table(steps, steps, NY, -1.0).T
    gx = np.concatenate([np.arange(0, NX, 2), np.arange(1, NX, 2)])
    xin = wave_table(np.arange(NX), gx, NX, 1.0)
    xout = wave_table(gx, np.arange(NX), NX, -1.0)
    dx, hx = derivative_matrix(NX), cas_matrix(NX)
    xmid = np.concatenate([dx.reshape(8, 8, NX), hx.reshape(8, 8, NX)], axis=1)
    dz = derivative_matrix(NZ)[:, 0]
    dz = np.concatenate([dz, dz, dz]).astype(np.float32)
    g_sq = squared_freq(NZ)[:, None, None] + squared_freq(NX)[None, :, None] + squared_freq(NY)[None, None, :]
    hart = np.where(g_sq > 0, 4.0 * np.pi / np.where(g_sq > 0, g_sq, 1.0), 0.0)
    along = np.real(np.fft.ifft(hart, axis=0))[: NZ // 2 + 1] / (NX * NY)
    along = along.reshape(65, 8, 8, NY).transpose(1, 0, 2, 3).astype(np.float32)
    return {
        "zin": two_parts(zin),
        "zout": two_parts(zout),
        "yin": two_parts(yin),
        "yout": two_parts(yout),
        "xin": two_parts(xin),
        "xout": two_parts(xout),
        "xmid": two_parts(xmid),
        "dy": two_parts(derivative_matrix(NY).T),
        "hy": two_parts(cas_matrix(NY)),
        "hx": two_parts(hx),
        "dz": dz,
        "along": along,
    }


def parts(values):
    high = values.astype(BF16)
    return high, (values - high.astype(F32)).astype(BF16)


def dot(a, b):
    return jnp.dot(a, b, preferred_element_type=F32)


def dot_t(a, b):
    return lax.dot_general(a, b, (((1,), (1,)), ((), ())), preferred_element_type=F32)


def table_first(table, values):
    high, low = parts(values)
    return dot(table[0], high) + dot(table[0], low) + dot(table[1], high)


def table_last(values, table):
    high, low = parts(values)
    return dot(high, table[0]) + dot(low, table[0]) + dot(high, table[1])


def meet(peers):
    barrier = pltpu.get_barrier_semaphore()
    for peer in peers:
        pl.semaphore_signal(barrier, inc=1, device_id=peer, device_id_type=MESH)
    return barrier


def exchange(src, dst, send_sem, recv_sem):
    me = lax.axis_index("plane")
    copies = []
    for step in range(1, PLANES):
        peer = lax.rem(me + step, PLANES)
        copy = pltpu.make_async_remote_copy(
            src_ref=src.at[peer],
            dst_ref=dst.at[me],
            send_sem=send_sem.at[step],
            recv_sem=recv_sem.at[step],
            device_id={"plane": peer},
            device_id_type=MESH,
        )
        copy.start()
        copies.append(copy)
    dst[me] = src[me]
    for copy in copies:
        copy.wait()


def sticks_kernel(coeffs, mask, zin, out, held, send_sem, recv_sem):
    me = lax.axis_index("plane")
    barrier = meet([{"plane": lax.rem(me + step, PLANES)} for step in range(1, PLANES)])
    keep = mask[...].astype(F32)
    values = (coeffs[...] * keep[None]).reshape(2 * NZ, CHUNK)
    held[...] = table_first(zin, values).reshape(PLANES, 32, CHUNK)
    pl.semaphore_wait(barrier, PLANES - 1)
    exchange(held, out, send_sem, recv_sem)


def back_kernel(picked, mask, zout, out, held, send_sem, recv_sem):
    me = lax.axis_index("plane")
    barrier = meet([{"plane": lax.rem(me + step, PLANES)} for step in range(1, PLANES)])
    pl.semaphore_wait(barrier, PLANES - 1)
    exchange(picked, held, send_sem, recv_sem)
    force = table_first(zout, held[...].reshape(256, CHUNK)).reshape(2, NZ, CHUNK)
    out[...] = force * mask[...].astype(F32)[None]


def one_hots(cols, chunk):
    col = cols[pl.ds(chunk, 1), :]
    upper, lower = col >> 8, col & 255
    rows = lax.broadcasted_iota(jnp.int32, (32, CHUNK), 0)
    above = jnp.where(rows == upper, 1.0, 0.0)
    rows = lax.broadcasted_iota(jnp.int32, (256, CHUNK), 0)
    below = jnp.where(rows == lower, 1.0, 0.0).astype(BF16)
    return above, below


def wave_kernel(sticks, cols, yin, xin, psi, density, grid, lines):
    for chunk in range(PLANES):
        above, below = one_hots(cols, chunk)
        above = above.astype(BF16)[None]
        high, low = parts(sticks[chunk])
        left = (high[:, None, :] * above).reshape(1024, CHUNK)
        total = dot_t(left, below)
        left = (low[:, None, :] * above).reshape(1024, CHUNK)
        total = total + dot_t(left, below)
        if chunk == 0:
            grid[...] = total
        else:
            grid[...] += total
    for odd in range(2):
        lanes = slice(odd * 128, odd * 128 + 128)
        rows = jnp.concatenate([grid[0:512, lanes], grid[512:1024, lanes]], axis=1)
        turned = table_last(rows, yin)
        for z in range(16):
            for c in range(2):
                first = c * 64 + odd * 32
                lines[first : first + 32, z * 128 : z * 128 + 128] = turned[
                    z * 32 : z * 32 + 32, c * 128 : c * 128 + 128
                ]
    wave = table_first(xin, lines[...])
    psi[...] = wave
    density[...] = (wave[:64] * wave[:64] + wave[64:] * wave[64:]) * (1.0 / STATES)


def force_kernel(psi, near, far, cols, hx, hy, xout, yout, picked, lines, grid):
    turned = table_first(hx, far[...])
    rows = jnp.concatenate([turned[:, z * 128 : z * 128 + 128] for z in range(16)], axis=0)
    turned = table_last(rows, hy)
    for z in range(16):
        lanes = slice(z * 128, z * 128 + 128)
        potential = near[:, lanes] + turned[z * 64 : z * 64 + 64]
        lines[0:64, lanes] = potential * psi[0:64, lanes]
        lines[64:128, lanes] = potential * psi[64:128, lanes]
    lines[...] = table_first(xout, lines[...])
    for odd in range(2):
        rows = jnp.concatenate(
            [
                jnp.concatenate(
                    [
                        lines[c * 64 + odd * 32 : c * 64 + odd * 32 + 32, z * 128 : z * 128 + 128]
                        for z in range(16)
                    ],
                    axis=0,
                )
                for c in range(2)
            ],
            axis=1,
        )
        turned = table_last(rows, yout)
        lanes = slice(odd * 128, odd * 128 + 128)
        grid[0:512, lanes] = turned[:, 0:128]
        grid[512:1024, lanes] = turned[:, 128:256]
    high, low = parts(grid[...])
    for chunk in range(PLANES):
        above, below = one_hots(cols, chunk)
        total = dot(high, below) + dot(low, below)
        picked[chunk] = jnp.sum(total.reshape(32, 32, CHUNK) * above[None], axis=1)


def xc_terms(rho, g):
    kappa, mu = 0.804, 0.2195
    exch = 0.75 * (3.0 / math.pi) ** (1.0 / 3.0)
    scale = 1.0 / (4.0 * (3.0 * math.pi**2) ** (2.0 / 3.0))
    root = jnp.exp(jnp.log(rho) * (1.0 / 3.0))
    root = root - (root * root * root - rho) / (3.0 * root * root)
    four = rho * root
    s2 = scale * g / (four * four)
    q = 1.0 / (1.0 + s2 * (mu / kappa))
    enhance = 1.0 + kappa - kappa * q
    radius = (3.0 / (4.0 * math.pi)) ** (1.0 / 3.0) / root
    inverse = 1.0 / (7.8 + radius)
    v_local = -exch * root * ((4.0 / 3.0) * enhance - (8.0 / 3.0) * mu * s2 * q * q)
    v_local = v_local - 0.44 * inverse - (0.44 / 3.0) * radius * inverse * inverse
    return v_local, (-2.0 * exch * mu * scale) * q * q / four


def tiles(block):
    return jnp.concatenate([block[:, z * 128 : z * 128 + 128] for z in range(8)], axis=0)


def untile(rows):
    return jnp.concatenate([rows[z * 8 : z * 8 + 8] for z in range(8)], axis=1)


def along_z(source, home, weight):
    def body(other, sums):
        base = home - other * 8 + 128
        held = [source[other, :, z * 128 : z * 128 + 128] for z in range(8)]
        factors = {shift: weight(base + shift) for shift in range(-7, 8)}
        sums = list(sums)
        for to in range(8):
            for z in range(8):
                sums[to] = sums[to] + factors[to - z] * held[z]
        return tuple(sums)

    sums = lax.fori_loop(0, 16, body, tuple(jnp.zeros((8, 128), F32) for _ in range(8)))
    return jnp.concatenate(sums, axis=1)


def middle_kernel(
    partial, core, xmid, dy, hy, dz, along, near, far,
    given, block, flux_x, flux_z, rho_hat, near_own, far_own, by_x, by_x2, by_z, by_z2, by_z3, kernel_z,
    kernel_sem, send, recv,
):
    s, p = lax.axis_index("state"), lax.axis_index("plane")
    band, half = s // 2, lax.rem(s, 2)
    place = p * 2 + half

    fetch = pltpu.make_async_copy(along.at[band], kernel_z, kernel_sem)
    fetch.start()

    states = [lax.rem(s + step, 16) for step in range(1, 16)]
    bands = [lax.rem(band + step, 8) * 2 + half for step in range(1, 8)]
    places = [lax.rem(place + step, 16) for step in range(1, 16)]
    places = [{"state": band * 2 + lax.rem(other, 2), "plane": other // 2} for other in places]

    barrier = meet(
        [{"state": other, "plane": p} for other in states]
        + [
            {"state": band * 2 + part, "plane": lax.rem(p + step, 8)}
            for step in range(1, 8)
            for part in range(2)
        ]
    )
    pl.semaphore_wait(barrier, 29)

    count = [0]

    def post(src, dst, to):
        at = count[0]
        count[0] += 1
        copy = pltpu.make_async_remote_copy(
            src_ref=src, dst_ref=dst, send_sem=send.at[at], recv_sem=recv.at[at], device_id=to, device_id_type=MESH
        )
        copy.start()
        return copy

    def rows_of(other):
        return pl.ds(pl.multiple_of(other // 2 * 8, 8), 8)

    def lanes_of(other):
        return pl.ds(pl.multiple_of(lax.rem(other, 2) * 1024, 1024), 1024)

    copies = [
        post(partial.at[rows_of(other), lanes_of(other)], given.at[s], {"state": other, "plane": p})
        for other in states
    ]
    own = [core[half * 8 + z, rows_of(s), :] for z in range(8)]
    rho = jnp.concatenate(own, axis=1) + partial[rows_of(s), lanes_of(s)]
    for copy, other in zip(copies, range(1, 16)):
        copy.wait()
        rho = rho + given[lax.rem(s - other + 16, 16)]
    block[...] = rho

    def all_x(src, dst):
        return [post(src, dst.at[rows_of(s), :], {"state": other, "plane": p}) for other in bands]

    def all_z(src, dst):
        return [post(src, dst.at[place], to) for to in places]

    def done(copies):
        for copy in copies:
            copy.wait()

    x_copies, z_copies = all_x(block, by_x), all_z(block, by_z)
    by_x[rows_of(s), :] = rho
    by_z[place] = rho
    rows = tiles(rho)
    grad_y = untile(table_last(rows, dy))
    done(x_copies)
    high, low = parts(by_x[...])
    both = dot(xmid[0, band], high) + dot(xmid[0, band], low) + dot(xmid[1, band], high)
    grad_x, rho_x = both[:8], both[8:]
    rho_xy = untile(table_last(tiles(rho_x), hy))
    rho_hat[...] = rho_xy
    r_copies = all_z(rho_hat, by_z3)
    by_z3[place] = rho_xy
    done(z_copies)
    home = place * 8
    grad_z = along_z(by_z, home, lambda at: dz[at])
    v_local, twice = xc_terms(rho, grad_z * grad_z + grad_x * grad_x + grad_y * grad_y)
    flux = twice * grad_z
    flux_z[...] = flux
    z_copies = all_z(flux_z, by_z2)
    by_z2[place] = flux
    flux = twice * grad_x
    flux_x[...] = flux
    x_copies = all_x(flux_x, by_x2)
    by_x2[rows_of(s), :] = flux
    total = v_local - untile(table_last(tiles(twice * grad_y), dy))

    fetch.wait()
    done(r_copies)

    def weight(at):
        at = lax.rem(at, 128)
        return kernel_z[jnp.minimum(at, 128 - at)]

    spread = along_z(by_z3, home, weight)
    far_own[...] = spread

    def all_states(src, dst):
        return [
            post(src, dst.at[rows_of(s), lanes_of(s)], {"state": other, "plane": p}) for other in states
        ]

    f_copies = all_states(far_own, far)
    far[rows_of(s), lanes_of(s)] = spread
    done(x_copies)
    high, low = parts(by_x2[...])
    both = dot(xmid[0, band], high) + dot(xmid[0, band], low) + dot(xmid[1, band], high)
    total = total - both[:8]
    done(z_copies)
    total = total - along_z(by_z2, home, lambda at: dz[at])
    near_own[...] = total
    n_copies = all_states(near_own, near)
    near[rows_of(s), lanes_of(s)] = total
    done(f_copies)
    done(n_copies)


VM = pl.BlockSpec(memory_space=pltpu.VMEM)


def call(kernel, outs, ins, scratch, in_specs=None, collective=None):
    return pl.pallas_call(
        kernel,
        out_shape=[jax.ShapeDtypeStruct(shape, F32) for shape in outs],
        in_specs=in_specs or [VM] * len(ins),
        out_specs=[VM] * len(outs),
        scratch_shapes=scratch,
        compiler_params=pltpu.CompilerParams(
            collective_id=collective,
            has_side_effects=collective is not None,
            vmem_limit_bytes=VMEM_LIMIT,
        ),
    )(*ins)


def on_device(coeffs, mask, stick_cols, core):
    t = {name: jnp.asarray(table) for name, table in tables().items()}
    cols = stick_cols.reshape(PLANES, CHUNK)
    sems = [pltpu.SemaphoreType.DMA((PLANES,))] * 2
    sticks, = call(
        sticks_kernel,
        [(PLANES, 32, CHUNK)],
        [coeffs.reshape(2, NZ, CHUNK), mask, t["zin"]],
        [pltpu.VMEM((PLANES, 32, CHUNK), F32), *sems],
        collective=0,
    )
    psi, partial = call(
        wave_kernel,
        [(128, 2048), (64, 2048)],
        [sticks, cols, t["yin"], t["xin"]],
        [pltpu.VMEM((1024, 256), F32), pltpu.VMEM((128, 2048), F32)],
    )
    own = pltpu.VMEM((8, 1024), F32)
    near, far = call(
        middle_kernel,
        [(64, 2048), (64, 2048)],
        [partial, core, t["xmid"], t["dy"], t["hy"], t["dz"], t["along"]],
        [
            pltpu.VMEM((16, 8, 1024), F32), own, own, own, own, own, own,
            pltpu.VMEM((64, 1024), F32), pltpu.VMEM((64, 1024), F32),
            pltpu.VMEM((16, 8, 1024), F32), pltpu.VMEM((16, 8, 1024), F32), pltpu.VMEM((16, 8, 1024), F32),
            pltpu.VMEM((65, 8, 128), F32),
            pltpu.SemaphoreType.DMA,
            pltpu.SemaphoreType.DMA((104,)),
            pltpu.SemaphoreType.DMA((104,)),
        ],
        in_specs=[VM] * 5 + [pl.BlockSpec(memory_space=pltpu.SMEM), pl.BlockSpec(memory_space=pl.ANY)],
        collective=1,
    )
    picked, = call(
        force_kernel,
        [(PLANES, 32, CHUNK)],
        [psi, near, far, cols, t["hx"], t["hy"], t["xout"], t["yout"]],
        [pltpu.VMEM((128, 2048), F32), pltpu.VMEM((1024, 256), F32)],
    )
    forces, = call(
        back_kernel,
        [(2, NZ, CHUNK)],
        [picked, mask, t["zout"]],
        [pltpu.VMEM((PLANES, 32, CHUNK), F32), *sems],
        collective=2,
    )
    return forces.reshape(2, 1, NZ, CHUNK)


def solution(mesh):
    in_specs = (P(None, "state", None, "plane"), P(None, "plane"), P(), P("plane", None, None))
    out_specs = P(None, "state", None, "plane")
    return jax.shard_map(
        on_device, mesh=mesh, in_specs=in_specs, out_specs=out_specs, check_vma=False
    )
```

time: 907 us -> 103 us (0.11)
  local copies, waits for them, and re-layouts: 572 us -> 3.07 us
  other arithmetic: 106 us -> 0 us
  Pallas kernels: 0 us -> 99.6 us
  waiting for transfers between devices: 94.8 us -> 0 us
  blocking collectives: 47.6 us -> 0 us
  matrix products: 36 us -> 0 us
  starting transfers between devices: 28.3 us -> 0 us
  between operations: 14.6 us -> 0.03 us
    scatter x1 -> x0, local copies, waits for them, and re-layouts: 280 us -> none  [on_device(): empty.at[:, :, :, stick_cols].set(sent)]
    slice x10 -> x0, local copies, waits for them, and re-layouts: 156 us -> none  [the longest x2 143 us: grid_forward(): return rotate(turned[0], turned[1], pcos, psin, -1.0, 'mpq,pk->mkq')]
    pallas_call x0 -> x5, Pallas kernels: none -> 99.6 us  [call(): pl.pallas_call(kernel, out_shape=[jax.ShapeDtypeStruct(shape, F32) for sh...]
    unnamed x5 -> x0, other arithmetic: 93.9 us -> none
    reduce_scatter x1 -> x0, waiting for transfers between devices: 56.5 us -> none  [on_device(): lax.psum_scatter(partial_value, 'state', scatter_dimension=0, tiled=True)]
    unnamed x20 -> x1, local copies, waits for them, and re-layouts: 52.9 us -> 1.77 us
    another operation x19 -> x0, local copies, waits for them, and re-layouts: 41.3 us -> none  [the longest x5 25.4 us: grid_forward(): flat = jnp.stack([breal, bimag]).reshape(2, count, local_planes, NX * NY)]
    all_to_all x4 -> x0, waiting for transfers between devices: 38.2 us -> none  [the longest x2 20.3 us: grid_forward(): lax.all_to_all(flat, ('state', 'plane'), split_axis=3, concat_axis=2, til...]
  transfers between devices with their start and end apart: 5 -> 0, of which waited for: 5 -> 0; matrix products, arithmetic and copies ran while one was open for 0% -> 0% of each run, Pallas kernels for 0% -> 0%
where the time goes in v1:
time: 103 us
  Pallas kernels  99.6 us (97%)
  local copies, waits for them, and re-layouts  3.07 us (3%)
    pallas_call x5, Pallas kernels, call(): pl.pallas_call(kernel, out_shape=[jax.ShapeDtypeStruct(shape, F32) for sh...  99.6 us

profile of v1, /device:TPU:1, one launch (start us, length us, event | category | flops | bytes accessed | tf_op | source)
XLA Modules:
  0.0 102.7 jit_solution(2349702313911147548)
XLA Ops:
  0.0 1.3 %reshape.10.cols = s32[8,384]{1,0:T(8,128)} reshape(s32[3072]{0:T(1024)} %param.18) | data formatting | bytes 24576 | tf_op jit(solution)/shard_map/reshape | solution.py:419
  1.3 15.6 %shard_map.154.sticks = f32[8,32,384]{2,1,0:T(8,128)} custom-call(f32[2,128,384]{2,1,0:T(8,128)} %bitcast.5, s32[128,384]{1,0:T(8,128)} %mask.3, bf16[2,256,256]{2,1,0:T(8,128)(2,1)} %constant.24.clone.zin), custom_call_target="tpu_custom_call" | custom-call | tf_op jit(solution)/shard_map/pallas_call | solution.py:403
  17.0 9.3 %shard_map.155 = (f32[128,2048]{1,0:T(8,128)}, f32[64,2048]{1,0:T(8,128)}) custom-call(f32[8,32,384]{2,1,0:T(8,128)} %shard_map.154.sticks, s32[8,384]{1,0:T(8,128)} %reshape.10.cols, bf16[2,256,256]{2,1,0:T(8,128)(2,1)} %constant.26.clone.yin, bf16[2,128,128]{2,1,0:T(8,128)(2,1)} %constant.28.clone.xin), custom_call_target="tpu_custom_call" | custom-call | tf_op jit(solution)/shard_map/pallas_call | solution.py:403
  26.3 54.0 %shard_map.156 = (f32[64,2048]{1,0:T(8,128)}, f32[64,2048]{1,0:T(8,128)}) custom-call(f32[64,2048]{1,0:T(8,128)} %get-tuple-element.10.partial, f32[16,64,128]{2,1,0:T(8,128)} %core.1, bf16[2,8,16,64]{3,2,1,0:T(8,128)(2,1)} %constant.30.clone.xmid, bf16[2,128,128]{2,1,0:T(8,128)(2,1)} %constant.31.clone.dy, bf16[2,128,128]{2,1,0:T(8,128)(2,1)} %constant.32.clone.hy, ...), custom_call_target="tpu_custom_call" | custom-call | tf_op jit(solution)/shard_map/pallas_call | solution.py:403
  80.2 9.5 %shard_map.157.picked = f32[8,32,384]{2,1,0:T(8,128)} custom-call(f32[128,2048]{1,0:T(8,128)} %get-tuple-element.9.psi, f32[64,2048]{1,0:T(8,128)} %get-tuple-element.11.near, f32[64,2048]{1,0:T(8,128)} %get-tuple-element.12.far, s32[8,384]{1,0:T(8,128)} %reshape.10.cols, bf16[2,64,64]{2,1,0:T(8,128)(2,1)} %constant.33.clone.hx, ...), custom_call_target="tpu_custom_call" | custom-call | tf_op jit(solution)/shard_map/pallas_call | solution.py:403
  89.8 11.2 %shard_map.158 = f32[2,128,384]{2,1,0:T(8,128)} custom-call(f32[8,32,384]{2,1,0:T(8,128)} %shard_map.157.picked, s32[128,384]{1,0:T(8,128)} %mask.3, bf16[2,256,256]{2,1,0:T(8,128)(2,1)} %constant.25.clone.zout), custom_call_target="tpu_custom_call" | custom-call | tf_op jit(solution)/shard_map/pallas_call | solution.py:403
  101.0 1.8 %copy.19 = f32[2,1,128,384]{3,2,1,0:T(8,128)} copy(f32[2,1,128,384]{3,2,1,0:T(8,128)} %bitcast.4) | data formatting | bytes 786432

commit v2 on v1

v2 whole, which is shorter than its diff:
```python
import functools
import math

import jax
import jax.numpy as jnp
import ml_dtypes
import numpy as np
from jax import lax
from jax.experimental import pallas as pl
from jax.experimental.pallas import tpu as pltpu
from jax.sharding import PartitionSpec as P

NZ = 128
NX = 64
NY = 128
NSTICK = 3072
STATES = 16
PLANES = 8
CHUNK = NSTICK // PLANES
SPACING = 0.5
CELLS = NX * NY * NZ
NORM = 1.0 / math.sqrt(4.0 * NSTICK * NZ)
F32 = jnp.float32
BF16 = jnp.bfloat16
MESH = pl.DeviceIdType.MESH
VMEM_LIMIT = 60 * 1024 * 1024


def two_parts(table):
    high = np.asarray(table, np.float64).astype(ml_dtypes.bfloat16)
    low = (np.asarray(table, np.float64) - high.astype(np.float64)).astype(ml_dtypes.bfloat16)
    return np.stack([high, low])


def wave_table(out_freq, in_freq, count, sign):
    angle = 2.0 * np.pi * (np.outer(out_freq, in_freq) % count) / count
    cos, sin = np.cos(angle), sign * np.sin(angle)
    return np.block([[cos, -sin], [sin, cos]])


def derivative_matrix(count):
    signed = np.arange(count)
    signed = np.where(signed >= count // 2, signed - count, signed)
    deriv = np.where(signed == -(count // 2), 0, signed) * 2.0 * np.pi / (count * SPACING)
    return np.real(np.fft.ifft(1j * deriv[:, None] * np.fft.fft(np.eye(count), axis=0), axis=0))


def cas_matrix(count):
    angle = 2.0 * np.pi * (np.outer(np.arange(count), np.arange(count)) % count) / count
    return np.cos(angle) + np.sin(angle)


def squared_freq(count):
    signed = np.arange(count)
    signed = np.where(signed >= count // 2, signed - count, signed)
    return (signed * 2.0 * np.pi / (count * SPACING)) ** 2


@functools.cache
def tables():
    steps = np.arange(128)
    zwave = wave_table(steps, steps, NZ, 1.0).reshape(2, PLANES, 16, 256)
    zin = NORM * zwave.transpose(1, 0, 2, 3).reshape(256, 256)
    zwave = wave_table(steps, steps, NZ, -1.0).reshape(256, 2, PLANES, 16)
    zout = -zwave.transpose(0, 2, 1, 3).reshape(256, 256) / (CELLS * NORM)
    yin = wave_table(steps, steps, NY, 1.0).T
    yout = wave_table(steps, steps, NY, -1.0).T
    gx = np.concatenate([np.arange(0, NX, 2), np.arange(1, NX, 2)])
    xin = wave_table(np.arange(NX), gx, NX, 1.0)
    xout = wave_table(gx, np.arange(NX), NX, -1.0)
    dx, hx = derivative_matrix(NX), cas_matrix(NX)
    xmid = np.concatenate([dx.reshape(8, 8, NX), hx.reshape(8, 8, NX)], axis=1)
    dz = derivative_matrix(NZ)[:, 0]
    dz = np.concatenate([dz, dz, dz]).astype(np.float32)
    g_sq = squared_freq(NZ)[:, None, None] + squared_freq(NX)[None, :, None] + squared_freq(NY)[None, None, :]
    hart = np.where(g_sq > 0, 4.0 * np.pi / np.where(g_sq > 0, g_sq, 1.0), 0.0)
    along = np.real(np.fft.ifft(hart, axis=0))[: NZ // 2 + 1] / (NX * NY)
    along = along.reshape(65, 8, 8, NY).transpose(1, 0, 2, 3).astype(np.float32)
    return {
        "zin": two_parts(zin),
        "zout": two_parts(zout),
        "yin": two_parts(yin),
        "yout": two_parts(yout),
        "xin": two_parts(xin),
        "xout": two_parts(xout),
        "xmid": two_parts(xmid),
        "dy": two_parts(derivative_matrix(NY).T),
        "hy": two_parts(cas_matrix(NY)),
        "hx": two_parts(hx),
        "dz": dz,
        "along": along,
    }


def parts(values):
    high = values.astype(BF16)
    return high, (values - high.astype(F32)).astype(BF16)


def dot(a, b):
    return jnp.dot(a, b, preferred_element_type=F32)


def dot_t(a, b):
    return lax.dot_general(a, b, (((1,), (1,)), ((), ())), preferred_element_type=F32)


def table_first(table, values):
    high, low = parts(values)
    return dot(table[0], high) + dot(table[0], low) + dot(table[1], high)


def table_last(values, table):
    high, low = parts(values)
    return dot(high, table[0]) + dot(low, table[0]) + dot(high, table[1])


def one_hot(values, rows):
    places = lax.broadcasted_iota(jnp.int32, (rows, values.shape[1]), 0)
    return jnp.where(places == values, 1.0, 0.0)


def columns_of(cols, chunk):
    return cols[:, pl.ds(pl.multiple_of(chunk * CHUNK, 128), CHUNK)]


def xc_terms(rho, g):
    kappa, mu = 0.804, 0.2195
    exch = 0.75 * (3.0 / math.pi) ** (1.0 / 3.0)
    scale = 1.0 / (4.0 * (3.0 * math.pi**2) ** (2.0 / 3.0))
    root = jnp.exp(jnp.log(rho) * (1.0 / 3.0))
    root = root - (root * root * root - rho) / (3.0 * root * root)
    four = rho * root
    s2 = scale * g / (four * four)
    q = 1.0 / (1.0 + s2 * (mu / kappa))
    enhance = 1.0 + kappa - kappa * q
    radius = (3.0 / (4.0 * math.pi)) ** (1.0 / 3.0) / root
    inverse = 1.0 / (7.8 + radius)
    v_local = -exch * root * ((4.0 / 3.0) * enhance - (8.0 / 3.0) * mu * s2 * q * q)
    v_local = v_local - 0.44 * inverse - (0.44 / 3.0) * radius * inverse * inverse
    return v_local, (-2.0 * exch * mu * scale) * q * q / four


def tiles(block, count):
    return jnp.concatenate([block[:, z * 128 : z * 128 + 128] for z in range(8)], axis=0)


def untile(rows, count):
    return jnp.concatenate([rows[z * count : z * count + count] for z in range(8)], axis=1)


def along_z(source, base, weight):
    def body(other, sums):
        start = base - other * 16
        held = [source[other, :, z * 128 : z * 128 + 128] for z in range(8)]
        factors = {shift: weight(start + shift) for shift in range(-7, 8)}
        sums = list(sums)
        for to in range(8):
            for z in range(8):
                sums[to] = sums[to] + factors[to - z] * held[z]
        return tuple(sums)

    sums = lax.fori_loop(0, PLANES, body, tuple(jnp.zeros((8, 128), F32) for _ in range(8)))
    return jnp.concatenate(sums, axis=1)


STEPS = ((2, 1), (1, 1), (3, 1), (2, 0), (0, 1), (1, 0), (3, 0))


def partner(place, ring, pair):
    return lax.rem(place // 2 + ring, 4) * 2 + lax.rem(place + pair, 2)


def step_kernel(
    coeffs, mask, cols, core, zin, yin, xin, xmid, dy, hy, hx, xout, yout, dz, along,
    back,
    held, sticks, grid, lines, psi, partial, summed, given,
    block, flux_x, flux_z, rho_hat, near_own, far_own, to_twin, from_twin,
    by_x, by_x2, by_z, by_z2, by_z3, kernel_z, near, far, pot, pot_twin, picked,
    kernel_sem, send, recv,
):
    s, p = lax.axis_index("state"), lax.axis_index("plane")
    band, half = s // 2, lax.rem(s, 2)
    twin = 1 - half

    fetch = pltpu.make_async_copy(along.at[band], kernel_z, kernel_sem)
    fetch.start()

    def on_plane(ring, pair):
        return {"state": s, "plane": partner(p, ring, pair)}

    def on_band(ring, pair):
        return {"state": partner(band, ring, pair) * 2 + half, "plane": p}

    on_twin = {"state": band * 2 + twin, "plane": p}

    barrier = pltpu.get_barrier_semaphore()
    for to in [on_twin] + [on_plane(*step) for step in STEPS] + [on_band(*step) for step in STEPS]:
        pl.semaphore_signal(barrier, inc=1, device_id=to, device_id_type=MESH)

    count = [0]

    def post(src, dst, to):
        at = count[0]
        count[0] += 1
        copy = pltpu.make_async_remote_copy(
            src_ref=src, dst_ref=dst, send_sem=send.at[at], recv_sem=recv.at[at], device_id=to, device_id_type=MESH
        )
        copy.start()
        return copy

    def done(copies):
        for copy in copies:
            copy.wait()

    def rows_of(other):
        return pl.ds(pl.multiple_of(other * 8, 8), 8)

    def lanes_of(part):
        return pl.ds(pl.multiple_of(part * 1024, 1024), 1024)

    values = (coeffs[...] * mask[...].astype(F32)[None]).reshape(2 * NZ, CHUNK)
    held[...] = table_first(zin, values).reshape(PLANES, 32, CHUNK)
    pl.semaphore_wait(barrier, 15)
    copies = [post(held.at[partner(p, *step)], sticks.at[p], on_plane(*step)) for step in STEPS]
    sticks[p] = held[p]

    def place(chunk):
        col = columns_of(cols, chunk)
        above = one_hot(col >> 8, 32).astype(BF16)[None]
        below = one_hot(col & 255, 256).astype(BF16)
        high, low = parts(sticks[chunk])
        left = jnp.concatenate(
            [(part[:, None, :] * above).reshape(1024, CHUNK) for part in (high, low)], axis=1
        )
        return dot_t(left, jnp.concatenate([below, below], axis=1))

    grid[...] = place(p)
    for copy, (ring, pair) in reversed(list(zip(copies, STEPS))):
        copy.wait()
        grid[...] += place(partner(p, 4 - ring, pair))

    for odd in range(2):
        lanes = slice(odd * 128, odd * 128 + 128)
        rows = jnp.concatenate([grid[0:512, lanes], grid[512:1024, lanes]], axis=1)
        turned = table_last(rows, yin)
        for z in range(16):
            for c in range(2):
                first = c * 64 + odd * 32
                lines[first : first + 32, z * 128 : z * 128 + 128] = turned[
                    z * 32 : z * 32 + 32, c * 128 : c * 128 + 128
                ]

    def waves(part):
        wave = table_first(xin, lines[:, lanes_of(part)])
        psi[:, lanes_of(part)] = wave
        return (wave[:64] * wave[:64] + wave[64:] * wave[64:]) * (1.0 / STATES)

    to_twin[...] = waves(twin)
    copy = post(to_twin, from_twin, on_twin)
    own = waves(half)
    copy.wait()
    summed[...] = own + from_twin[...]

    copies = [post(summed.at[rows_of(partner(band, *step)), :], given.at[band], on_band(*step)) for step in STEPS]
    rho = jnp.concatenate([core[half * 8 + z, rows_of(band), :] for z in range(8)], axis=1)
    rho = rho + summed[rows_of(band), :]
    for copy, (ring, pair) in reversed(list(zip(copies, STEPS))):
        copy.wait()
        rho = rho + given[partner(band, 4 - ring, pair)]
    block[...] = rho

    def all_bands(src, dst):
        return [post(src, dst.at[rows_of(band), :], on_band(*step)) for step in STEPS]

    def all_planes(src, dst):
        return [post(src, dst.at[p], on_plane(*step)) for step in STEPS]

    def across(source, weight, slot):
        base = p * 16 + 128
        partial[slot, 0] = along_z(source, base + (twin - half) * 8, weight)
        copy = post(partial.at[slot, 0], partial.at[slot, 1], on_twin)
        total = along_z(source, base, weight)
        copy.wait()
        return total + partial[slot, 1]

    def slope(at):
        return dz[at]

    def mixed_x(source):
        high, low = parts(source[...])
        return dot(xmid[0, band], high) + dot(xmid[0, band], low) + dot(xmid[1, band], high)

    x_copies, z_copies = all_bands(block, by_x), all_planes(block, by_z)
    by_x[rows_of(band), :] = rho
    by_z[p] = rho
    grad_y = untile(table_last(tiles(rho, 8), dy), 8)
    done(x_copies)
    both = mixed_x(by_x)
    grad_x = both[:8]
    rho_xy = untile(table_last(tiles(both[8:], 8), hy), 8)
    rho_hat[...] = rho_xy
    r_copies = all_planes(rho_hat, by_z3)
    by_z3[p] = rho_xy
    done(z_copies)
    grad_z = across(by_z, slope, 0)

    v_local, twice = xc_terms(rho, grad_z * grad_z + grad_x * grad_x + grad_y * grad_y)
    flux = twice * grad_z
    flux_z[...] = flux
    z_copies = all_planes(flux_z, by_z2)
    by_z2[p] = flux
    flux = twice * grad_x
    flux_x[...] = flux
    x_copies = all_bands(flux_x, by_x2)
    by_x2[rows_of(band), :] = flux
    total = v_local - untile(table_last(tiles(twice * grad_y, 8), dy), 8)

    fetch.wait()
    done(r_copies)

    def even(at):
        at = lax.rem(at, 128)
        return kernel_z[jnp.minimum(at, 128 - at)]

    spread = across(by_z3, even, 1)
    far_own[...] = spread
    f_copies = all_bands(far_own, far)
    far[rows_of(band), :] = spread

    done(x_copies)
    total = total - mixed_x(by_x2)[:8]
    done(z_copies)
    total = total - across(by_z2, slope, 2)
    near_own[...] = total
    n_copies = all_bands(near_own, near)
    near[rows_of(band), :] = total

    done(f_copies)
    turned = untile(table_last(tiles(table_first(hx, far[...]), 64), hy), 64)
    done(n_copies)
    pot[...] = near[...] + turned
    copy = post(pot, pot_twin, on_twin)

    def forces(potential, part):
        lanes = lanes_of(part)
        wave = psi[:, lanes]
        wave = jnp.concatenate([potential * wave[:64], potential * wave[64:]], axis=0)
        wave = table_first(xout, wave)
        for odd in range(2):
            rows = []
            for c in range(2):
                first = c * 64 + odd * 32
                rows.append(
                    jnp.concatenate([wave[first : first + 32, z * 128 : z * 128 + 128] for z in range(8)], axis=0)
                )
            turned = table_last(jnp.concatenate(rows, axis=1), yout)
            for c in range(2):
                at = pl.ds(pl.multiple_of(c * 512 + part * 256, 256), 256)
                grid[at, odd * 128 : odd * 128 + 128] = turned[:, c * 128 : c * 128 + 128]

    forces(pot[...], half)
    copy.wait()
    forces(pot_twin[...], twin)

    high, low = parts(grid[...])
    left = jnp.concatenate([high, low], axis=1)
    copies = []
    order = STEPS + ((0, 0),)
    for first in range(0, PLANES, 2):
        steps = order[first : first + 2]
        owners = [partner(p, *step) for step in steps]
        col = jnp.concatenate([columns_of(cols, owner) for owner in owners], axis=1)
        above = one_hot(col >> 8, 32)[None]
        below = one_hot(col & 255, 256).astype(BF16)
        found = dot(left, jnp.concatenate([below, below], axis=0)).reshape(32, 32, 2 * CHUNK)
        found = jnp.sum(found * above, axis=1)
        for at, (step, owner) in enumerate(zip(steps, owners)):
            chunk = found[:, at * CHUNK : (at + 1) * CHUNK]
            if step == (0, 0):
                back[p] = chunk
            else:
                picked[owner] = chunk
                copies.append(post(picked.at[owner], back.at[p], on_plane(*step)))
    done(copies)


def last_kernel(back, mask, zout, out):
    force = table_first(zout, back[...].reshape(256, CHUNK)).reshape(2, NZ, CHUNK)
    out[...] = force * mask[...].astype(F32)[None]


VM = pl.BlockSpec(memory_space=pltpu.VMEM)
COPIES = 7 * 10 + 5


def call(kernel, outs, ins, scratch=(), in_specs=None, collective=None):
    return pl.pallas_call(
        kernel,
        out_shape=[jax.ShapeDtypeStruct(shape, F32) for shape in outs],
        in_specs=in_specs or [VM] * len(ins),
        out_specs=[VM] * len(outs),
        scratch_shapes=scratch,
        compiler_params=pltpu.CompilerParams(
            collective_id=collective,
            has_side_effects=collective is not None,
            vmem_limit_bytes=VMEM_LIMIT,
        ),
    )(*ins)


def on_device(coeffs, mask, stick_cols, core):
    t = {name: jnp.asarray(table) for name, table in tables().items()}
    names = ("zin", "yin", "xin", "xmid", "dy", "hy", "hx", "xout", "yout")
    bundle, own, all_x, all_z = (PLANES, 32, CHUNK), (8, 1024), (64, 1024), (PLANES, 8, 1024)
    shapes = [bundle, bundle, (1024, 256), (128, 2048), (128, 2048), (3, 2, 8, 1024), all_x, all_z]
    shapes += [own] * 6 + [all_x] * 2
    shapes += [all_x] * 2 + [all_z] * 3 + [(65, 8, 128)] + [all_x] * 4 + [bundle]
    back, = call(
        step_kernel,
        [bundle],
        [coeffs.reshape(2, NZ, CHUNK), mask, stick_cols.reshape(1, NSTICK), core]
        + [t[name] for name in names]
        + [t["dz"], t["along"]],
        [pltpu.VMEM(shape, F32) for shape in shapes]
        + [pltpu.SemaphoreType.DMA, pltpu.SemaphoreType.DMA((COPIES,)), pltpu.SemaphoreType.DMA((COPIES,))],
        in_specs=[VM] * 13 + [pl.BlockSpec(memory_space=pltpu.SMEM), pl.BlockSpec(memory_space=pl.ANY)],
        collective=0,
    )
    forces, = call(last_kernel, [(2, NZ, CHUNK)], [back, mask, t["zout"]])
    return forces.reshape(2, 1, NZ, CHUNK)


def solution(mesh):
    in_specs = (P(None, "state", None, "plane"), P(None, "plane"), P(), P("plane", None, None))
    out_specs = P(None, "state", None, "plane")
    return jax.shard_map(
        on_device, mesh=mesh, in_specs=in_specs, out_specs=out_specs, check_vma=False
    )
```

time: 103 us -> 72.3 us (0.70)
  Pallas kernels: 99.6 us -> 72.1 us
  local copies, waits for them, and re-layouts: 3.07 us -> 0 us
    pallas_call x5 -> x2, Pallas kernels: 99.6 us -> 72.1 us  [call(): pl.pallas_call(kernel, out_shape=[jax.ShapeDtypeStruct(shape, F32) for sh...]
    unnamed x1 -> x0, local copies, waits for them, and re-layouts: 1.77 us -> none
    reshape x1 -> x0, local copies, waits for them, and re-layouts: 1.3 us -> none  [on_device(): cols = stick_cols.reshape(PLANES, CHUNK)]
where the time goes in v2:
time: 72.3 us; the launch traced here: 72.2 us
  Pallas kernels  72.1 us (100%)
    pallas_call x2, Pallas kernels, call(): pl.pallas_call(kernel, out_shape=[jax.ShapeDtypeStruct(shape, F32) for sh...  72.1 us

profile of v2, /device:TPU:1, one launch (start us, length us, event | category | flops | bytes accessed | tf_op | source)
XLA Modules:
  0.0 72.2 jit_solution(12973974156127464447)
XLA Ops:
  0.0 69.8 %shard_map.154.back = f32[8,32,384]{2,1,0:T(8,128)} custom-call(f32[2,128,384]{2,1,0:T(8,128)} %bitcast.5, s32[128,384]{1,0:T(8,128)} %mask.3, s32[1,3072]{1,0:T(1,128)} %bitcast.6, f32[16,64,128]{2,1,0:T(8,128)} %core.1, bf16[2,256,256]{2,1,0:T(8,128)(2,1)} %constant.24.clone.zin, bf16[2,256,256]{2,1,0:T(8,128)(2,1)} %constant.26.clone.yin, ...), custom_call_target="tpu_custom_call" | custom-call | tf_op jit(solution)/shard_map/pallas_call | solution.py:398
  69.8 2.3 %shard_map.155 = f32[2,128,384]{2,1,0:T(8,128)} custom-call(f32[8,32,384]{2,1,0:T(8,128)} %shard_map.154.back, s32[128,384]{1,0:T(8,128)} %mask.3, bf16[2,256,256]{2,1,0:T(8,128)(2,1)} %constant.25.clone.zout), custom_call_target="tpu_custom_call" | custom-call | tf_op jit(solution)/shard_map/pallas_call | solution.py:398

commit v3 on v2

--- a/solution.py
+++ b/solution.py
@@ -23,7 +23,6 @@
 F32 = jnp.float32
 BF16 = jnp.bfloat16
 MESH = pl.DeviceIdType.MESH
-VMEM_LIMIT = 60 * 1024 * 1024
 
 
 def two_parts(table):
@@ -54,6 +53,11 @@
     signed = np.arange(count)
     signed = np.where(signed >= count // 2, signed - count, signed)
     return (signed * 2.0 * np.pi / (count * SPACING)) ** 2
+
+
+def four_parts(table):
+    high, low = two_parts(table)
+    return np.block([[high, high], [low, low]])
 
 
 @functools.cache
@@ -81,12 +85,12 @@
         "zout": two_parts(zout),
         "yin": two_parts(yin),
         "yout": two_parts(yout),
-        "xin": two_parts(xin),
-        "xout": two_parts(xout),
+        "xin": four_parts(xin),
+        "xout": four_parts(xout),
         "xmid": two_parts(xmid),
         "dy": two_parts(derivative_matrix(NY).T),
         "hy": two_parts(cas_matrix(NY)),
-        "hx": two_parts(hx),
+        "hx": four_parts(hx),
         "dz": dz,
         "along": along,
     }
@@ -108,6 +112,12 @@
 def table_first(table, values):
     high, low = parts(values)
     return dot(table[0], high) + dot(table[0], low) + dot(table[1], high)
+
+
+def four_first(table, values):
+    both = dot(table[...], jnp.concatenate(parts(values), axis=0))
+    half = table.shape[0] // 2
+    return both[:half] + both[half:]
 
 
 def table_last(values, table):
@@ -149,21 +159,6 @@
     return jnp.concatenate([rows[z * count : z * count + count] for z in range(8)], axis=1)
 
 
-def along_z(source, base, weight):
-    def body(other, sums):
-        start = base - other * 16
-        held = [source[other, :, z * 128 : z * 128 + 128] for z in range(8)]
-        factors = {shift: weight(start + shift) for shift in range(-7, 8)}
-        sums = list(sums)
-        for to in range(8):
-            for z in range(8):
-                sums[to] = sums[to] + factors[to - z] * held[z]
-        return tuple(sums)
-
-    sums = lax.fori_loop(0, PLANES, body, tuple(jnp.zeros((8, 128), F32) for _ in range(8)))
-    return jnp.concatenate(sums, axis=1)
-
-
 STEPS = ((2, 1), (1, 1), (3, 1), (2, 0), (0, 1), (1, 0), (3, 0))
 
 
@@ -171,21 +166,26 @@
     return lax.rem(place // 2 + ring, 4) * 2 + lax.rem(place + pair, 2)
 
 
-def step_kernel(
-    coeffs, mask, cols, core, zin, yin, xin, xmid, dy, hy, hx, xout, yout, dz, along,
-    back,
-    held, sticks, grid, lines, psi, partial, summed, given,
+FIRST = ("coeffs", "mask", "zin")
+LOADED = FIRST + ("cols", "dz", "yin", "xin", "core", "xmid", "dy", "hy", "hx", "xout", "yout")
+
+
+def step_kernel(along, *refs):
+    away, (back, *refs) = refs[: len(LOADED)], refs[len(LOADED) :]
+    work(along, away, back, refs[: len(LOADED)], *refs[len(LOADED) :])
+
+
+def work(
+    along, away, back, near_by,
+    held, sticks, grid, psi, partial, summed, given,
     block, flux_x, flux_z, rho_hat, near_own, far_own, to_twin, from_twin,
     by_x, by_x2, by_z, by_z2, by_z3, kernel_z, near, far, pot, pot_twin, picked,
-    kernel_sem, send, recv,
+    kernel_sem, load_sem, send, recv,
 ):
     s, p = lax.axis_index("state"), lax.axis_index("plane")
     band, half = s // 2, lax.rem(s, 2)
     twin = 1 - half
 
-    fetch = pltpu.make_async_copy(along.at[band], kernel_z, kernel_sem)
-    fetch.start()
-
     def on_plane(ring, pair):
         return {"state": s, "plane": partner(p, ring, pair)}
 
@@ -197,6 +197,17 @@
     barrier = pltpu.get_barrier_semaphore()
     for to in [on_twin] + [on_plane(*step) for step in STEPS] + [on_band(*step) for step in STEPS]:
         pl.semaphore_signal(barrier, inc=1, device_id=to, device_id_type=MESH)
+
+    loads = {}
+    for at, name in enumerate(LOADED):
+        loads[name] = pltpu.make_async_copy(away[at], near_by[at], load_sem.at[at])
+    for name in FIRST:
+        loads[name].start()
+
+    def loaded(*names):
+        for name in names:
+            loads[name].wait()
+        return [near_by[LOADED.index(name)] for name in names]
 
     count = [0]
 
@@ -219,40 +230,58 @@
     def lanes_of(part):
         return pl.ds(pl.multiple_of(part * 1024, 1024), 1024)
 
+    coeffs, mask, zin = loaded("coeffs", "mask", "zin")
+    for name in LOADED[len(FIRST) :]:
+        loads[name].start()
+    fetch = pltpu.make_async_copy(along.at[band], kernel_z, kernel_sem)
+    fetch.start()
     values = (coeffs[...] * mask[...].astype(F32)[None]).reshape(2 * NZ, CHUNK)
     held[...] = table_first(zin, values).reshape(PLANES, 32, CHUNK)
     pl.semaphore_wait(barrier, 15)
     copies = [post(held.at[partner(p, *step)], sticks.at[p], on_plane(*step)) for step in STEPS]
     sticks[p] = held[p]
 
-    def place(chunk):
+    cols, = loaded("cols")
+
+    def place(chunk, fresh):
         col = columns_of(cols, chunk)
         above = one_hot(col >> 8, 32).astype(BF16)[None]
         below = one_hot(col & 255, 256).astype(BF16)
         high, low = parts(sticks[chunk])
-        left = jnp.concatenate(
-            [(part[:, None, :] * above).reshape(1024, CHUNK) for part in (high, low)], axis=1
-        )
-        return dot_t(left, jnp.concatenate([below, below], axis=1))
-
-    grid[...] = place(p)
+        below = jnp.concatenate([below, below], axis=1)
+        for first in (0, 16):
+            left = jnp.concatenate(
+                [(part[first : first + 16, None, :] * above).reshape(512, CHUNK) for part in (high, low)], axis=1
+            )
+            rows = slice(first * 32, first * 32 + 512)
+            if fresh:
+                grid[rows] = dot_t(left, below)
+            else:
+                grid[rows] += dot_t(left, below)
+
+    place(p, True)
     for copy, (ring, pair) in reversed(list(zip(copies, STEPS))):
         copy.wait()
-        grid[...] += place(partner(p, 4 - ring, pair))
-
-    for odd in range(2):
-        lanes = slice(odd * 128, odd * 128 + 128)
-        rows = jnp.concatenate([grid[0:512, lanes], grid[512:1024, lanes]], axis=1)
-        turned = table_last(rows, yin)
-        for z in range(16):
-            for c in range(2):
-                first = c * 64 + odd * 32
-                lines[first : first + 32, z * 128 : z * 128 + 128] = turned[
-                    z * 32 : z * 32 + 32, c * 128 : c * 128 + 128
+        place(partner(p, 4 - ring, pair), False)
+
+    yin, xin, core, xmid = loaded("yin", "xin", "core", "xmid")
+    def waves(part):
+        lines = []
+        for odd in range(2):
+            rows = [
+                grid[pl.ds(pl.multiple_of(c * 512 + part * 256, 256), 256), odd * 128 : odd * 128 + 128] for c in range(2)
+            ]
+            turned = table_last(jnp.concatenate(rows, axis=1), yin)
+            lines.append(
+                [
+                    jnp.concatenate(
+                        [turned[z * 32 : z * 32 + 32, c * 128 : c * 128 + 128] for z in range(8)], axis=1
+                    )
+                    for c in range(2)
                 ]
-
-    def waves(part):
-        wave = table_first(xin, lines[:, lanes_of(part)])
+            )
+        lines = jnp.concatenate([lines[odd][c] for c in range(2) for odd in range(2)], axis=0)
+        wave = four_first(xin, lines)
         psi[:, lanes_of(part)] = wave
         return (wave[:64] * wave[:64] + wave[64:] * wave[64:]) * (1.0 / STATES)
 
@@ -276,13 +305,36 @@
     def all_planes(src, dst):
         return [post(src, dst.at[p], on_plane(*step)) for step in STEPS]
 
-    def across(source, weight, slot):
-        base = p * 16 + 128
-        partial[slot, 0] = along_z(source, base + (twin - half) * 8, weight)
-        copy = post(partial.at[slot, 0], partial.at[slot, 1], on_twin)
-        total = along_z(source, base, weight)
-        copy.wait()
-        return total + partial[slot, 1]
+    class Along:
+        def __init__(self, copies, source, weight, slot):
+            self.arrivals = list(reversed(list(zip(copies, STEPS))))
+            self.source, self.weight, self.slot = source, weight, slot
+            self.sums = [[jnp.zeros((8, 128), F32)] * 8 for _ in range(2)]
+            self.add(p)
+
+        def add(self, other):
+            held = [self.source[other, :, z * 128 : z * 128 + 128] for z in range(8)]
+            for sums, part in zip(self.sums, (half, twin)):
+                start = (p - other) * 16 + (part - half) * 8 + 128
+                factors = {shift: self.weight(start + shift) for shift in range(-7, 8)}
+                for to in range(8):
+                    for z in range(8):
+                        sums[to] = sums[to] + factors[to - z] * held[z]
+
+        def take(self, number):
+            for copy, (ring, pair) in self.arrivals[:number]:
+                copy.wait()
+                self.add(partner(p, 4 - ring, pair))
+            self.arrivals = self.arrivals[number:]
+
+        def swap(self):
+            self.take(len(self.arrivals))
+            partial[self.slot, 0] = jnp.concatenate(self.sums[1], axis=1)
+            self.copy = post(partial.at[self.slot, 0], partial.at[self.slot, 1], on_twin)
+
+        def result(self):
+            self.copy.wait()
+            return jnp.concatenate(self.sums[0], axis=1) + partial[self.slot, 1]
 
     def slope(at):
         return dz[at]
@@ -291,10 +343,13 @@
         high, low = parts(source[...])
         return dot(xmid[0, band], high) + dot(xmid[0, band], low) + dot(xmid[1, band], high)
 
-    x_copies, z_copies = all_bands(block, by_x), all_planes(block, by_z)
+    dz, dy, hy, hx, xout, yout = loaded("dz", "dy", "hy", "hx", "xout", "yout")
     by_x[rows_of(band), :] = rho
     by_z[p] = rho
+    z_copies, x_copies = all_planes(block, by_z), all_bands(block, by_x)
+    grad_z = Along(z_copies, by_z, slope, 0)
     grad_y = untile(table_last(tiles(rho, 8), dy), 8)
+    grad_z.take(3)
     done(x_copies)
     both = mixed_x(by_x)
     grad_x = both[:8]
@@ -302,8 +357,15 @@
     rho_hat[...] = rho_xy
     r_copies = all_planes(rho_hat, by_z3)
     by_z3[p] = rho_xy
-    done(z_copies)
-    grad_z = across(by_z, slope, 0)
+    grad_z.swap()
+    fetch.wait()
+
+    def even(at):
+        at = lax.rem(at, 128)
+        return kernel_z[jnp.minimum(at, 128 - at)]
+
+    spread = Along(r_copies, by_z3, even, 1)
+    grad_z = grad_z.result()
 
     v_local, twice = xc_terms(rho, grad_z * grad_z + grad_x * grad_x + grad_y * grad_y)
     flux = twice * grad_z
@@ -316,28 +378,23 @@
     by_x2[rows_of(band), :] = flux
     total = v_local - untile(table_last(tiles(twice * grad_y, 8), dy), 8)
 
-    fetch.wait()
-    done(r_copies)
-
-    def even(at):
-        at = lax.rem(at, 128)
-        return kernel_z[jnp.minimum(at, 128 - at)]
-
-    spread = across(by_z3, even, 1)
+    slant = Along(z_copies, by_z2, slope, 2)
+    spread.swap()
+    slant.take(3)
+    spread = spread.result()
     far_own[...] = spread
     f_copies = all_bands(far_own, far)
     far[rows_of(band), :] = spread
-
+    slant.swap()
     done(x_copies)
     total = total - mixed_x(by_x2)[:8]
-    done(z_copies)
-    total = total - across(by_z2, slope, 2)
+    total = total - slant.result()
     near_own[...] = total
     n_copies = all_bands(near_own, near)
     near[rows_of(band), :] = total
 
     done(f_copies)
-    turned = untile(table_last(tiles(table_first(hx, far[...]), 64), hy), 64)
+    turned = untile(table_last(tiles(four_first(hx, far[...]), 64), hy), 64)
     done(n_copies)
     pot[...] = near[...] + turned
     copy = post(pot, pot_twin, on_twin)
@@ -346,7 +403,7 @@
         lanes = lanes_of(part)
         wave = psi[:, lanes]
         wave = jnp.concatenate([potential * wave[:64], potential * wave[64:]], axis=0)
-        wave = table_first(xout, wave)
+        wave = four_first(xout, wave)
         for odd in range(2):
             rows = []
             for c in range(2):
@@ -373,14 +430,20 @@
         col = jnp.concatenate([columns_of(cols, owner) for owner in owners], axis=1)
         above = one_hot(col >> 8, 32)[None]
         below = one_hot(col & 255, 256).astype(BF16)
-        found = dot(left, jnp.concatenate([below, below], axis=0)).reshape(32, 32, 2 * CHUNK)
-        found = jnp.sum(found * above, axis=1)
+        below = jnp.concatenate([below, below], axis=0)
+        found = [
+            jnp.sum(dot(left[rows : rows + 512], below).reshape(16, 32, 2 * CHUNK) * above, axis=1)
+            for rows in (0, 512)
+        ]
+        found = jnp.concatenate(found, axis=0)
         for at, (step, owner) in enumerate(zip(steps, owners)):
             chunk = found[:, at * CHUNK : (at + 1) * CHUNK]
+            picked[owner] = chunk
             if step == (0, 0):
-                back[p] = chunk
+                fetch = pltpu.make_async_copy(picked.at[p], back.at[p], kernel_sem)
+                fetch.start()
+                copies.append(fetch)
             else:
-                picked[owner] = chunk
                 copies.append(post(picked.at[owner], back.at[p], on_plane(*step)))
     done(copies)
 
@@ -390,44 +453,55 @@
     out[...] = force * mask[...].astype(F32)[None]
 
 
-VM = pl.BlockSpec(memory_space=pltpu.VMEM)
 COPIES = 7 * 10 + 5
 
 
-def call(kernel, outs, ins, scratch=(), in_specs=None, collective=None):
+def call(kernel, outs, ins, in_specs, out_specs, scratch=(), collective=None, limit=60):
     return pl.pallas_call(
         kernel,
         out_shape=[jax.ShapeDtypeStruct(shape, F32) for shape in outs],
-        in_specs=in_specs or [VM] * len(ins),
-        out_specs=[VM] * len(outs),
+        in_specs=in_specs,
+        out_specs=out_specs,
         scratch_shapes=scratch,
         compiler_params=pltpu.CompilerParams(
             collective_id=collective,
             has_side_effects=collective is not None,
-            vmem_limit_bytes=VMEM_LIMIT,
+            vmem_limit_bytes=limit * 1024 * 1024,
         ),
     )(*ins)
 
 
 def on_device(coeffs, mask, stick_cols, core):
     t = {name: jnp.asarray(table) for name, table in tables().items()}
-    names = ("zin", "yin", "xin", "xmid", "dy", "hy", "hx", "xout", "yout")
+    t.update(coeffs=coeffs.reshape(2, NZ, CHUNK), mask=mask, cols=stick_cols.reshape(1, NSTICK), core=core)
     bundle, own, all_x, all_z = (PLANES, 32, CHUNK), (8, 1024), (64, 1024), (PLANES, 8, 1024)
-    shapes = [bundle, bundle, (1024, 256), (128, 2048), (128, 2048), (3, 2, 8, 1024), all_x, all_z]
+    shapes = [bundle, bundle, (1024, 256), (128, 2048), (3, 2, 8, 1024), all_x, all_z]
     shapes += [own] * 6 + [all_x] * 2
     shapes += [all_x] * 2 + [all_z] * 3 + [(65, 8, 128)] + [all_x] * 4 + [bundle]
+    anywhere, whole = pl.BlockSpec(memory_space=pl.ANY), pl.BlockSpec(memory_space=pltpu.VMEM)
     back, = call(
         step_kernel,
         [bundle],
-        [coeffs.reshape(2, NZ, CHUNK), mask, stick_cols.reshape(1, NSTICK), core]
-        + [t[name] for name in names]
-        + [t["dz"], t["along"]],
-        [pltpu.VMEM(shape, F32) for shape in shapes]
-        + [pltpu.SemaphoreType.DMA, pltpu.SemaphoreType.DMA((COPIES,)), pltpu.SemaphoreType.DMA((COPIES,))],
-        in_specs=[VM] * 13 + [pl.BlockSpec(memory_space=pltpu.SMEM), pl.BlockSpec(memory_space=pl.ANY)],
+        [t["along"]] + [t[name] for name in LOADED],
+        [anywhere] * (len(LOADED) + 1),
+        [anywhere],
+        [
+            (pltpu.SMEM if name == "dz" else pltpu.VMEM)(t[name].shape, t[name].dtype)
+            for name in LOADED
+        ]
+        + [pltpu.VMEM(shape, F32) for shape in shapes]
+        + [pltpu.SemaphoreType.DMA, pltpu.SemaphoreType.DMA((len(LOADED),))]
+        + [pltpu.SemaphoreType.DMA((COPIES,)), pltpu.SemaphoreType.DMA((COPIES,))],
         collective=0,
     )
-    forces, = call(last_kernel, [(2, NZ, CHUNK)], [back, mask, t["zout"]])
+    forces, = call(
+        last_kernel,
+        [(2, NZ, CHUNK)],
+        [back, mask, t["zout"]],
+        [whole] * 3,
+        [whole],
+        limit=8,
+    )
     return forces.reshape(2, 1, NZ, CHUNK)
 
 

time: 72.3 us -> 64.7 us (0.89)
  Pallas kernels: 72.1 us -> 63.5 us
  local copies, waits for them, and re-layouts: 0 us -> 1 us
    pallas_call x2, Pallas kernels: 72.1 us -> 63.5 us  [call(): pl.pallas_call(kernel, out_shape=[jax.ShapeDtypeStruct(shape, F32) for sh...]
    unnamed x0 -> x6, local copies, waits for them, and re-layouts: none -> 1 us
where the time goes in v3:
time: 64.7 us; the launch traced here: 64.5 us
  Pallas kernels  63.5 us (98%)
  local copies, waits for them, and re-layouts  1 us (2%)
    pallas_call x2, Pallas kernels, call(): pl.pallas_call(kernel, out_shape=[jax.ShapeDtypeStruct(shape, F32) for sh...  63.5 us

profile of v3, /device:TPU:1, one launch (start us, length us, event | category | flops | bytes accessed | tf_op | source)
XLA Modules:
  0.0 64.5 jit_solution(7141923397755134413)
XLA Ops:
  0.0 0.0 copy-start.1
  0.0 0.0 copy-start.2
  0.0 62.3 %shard_map.154.back = f32[8,32,384]{2,1,0:T(8,128)} custom-call(f32[8,65,8,128]{3,2,1,0:T(8,128)} %constant.35.clone.along, f32[2,128,384]{2,1,0:T(8,128)} %bitcast.5, s32[128,384]{1,0:T(8,128)} %mask.1, bf16[2,256,256]{2,1,0:T(8,128)(2,1)} %constant.24.clone.refs_2_, s32[1,3072]{1,0:T(1,128)} %bitcast.6, f32[384]{0:T(512)} %constant.34.clone.refs_4_, ...), custom_call_target="tpu_custom_call" | custom-call | tf_op jit(solution)/shard_map/pallas_call | solution.py:460
  62.3 0.0 copy-done.1
  62.4 0.0 copy-done.2
  62.4 0.0 copy-start
  62.4 1.0 %copy-done = f32[8,32,384]{2,1,0:T(8,128)S(1)} copy-done((f32[8,32,384]{2,1,0:T(8,128)S(1)}, f32[8,32,384]{2,1,0:T(8,128)}, u32[]{:S(2)}) %copy-start) | copy-done | bytes 393240
  63.4 1.1 %shard_map.155 = f32[2,128,384]{2,1,0:T(8,128)} custom-call(f32[8,32,384]{2,1,0:T(8,128)S(1)} %copy-done, s32[128,384]{1,0:T(8,128)S(1)} %copy-done.1, bf16[2,256,256]{2,1,0:T(8,128)(2,1)S(1)} %copy-done.2), custom_call_target="tpu_custom_call" | custom-call | tf_op jit(solution)/shard_map/pallas_call | solution.py:460
Async XLA Ops:
  0.0 62.3 %copy-start.1 = (s32[128,384]{1,0:T(8,128)S(1)}, s32[128,384]{1,0:T(8,128)}, u32[]{:S(2)}) copy-start(s32[128,384]{1,0:T(8,128)} %mask.1) | copy-start | bytes 589828
  0.0 62.4 %copy-start.2 = (bf16[2,256,256]{2,1,0:T(8,128)(2,1)S(1)}, bf16[2,256,256]{2,1,0:T(8,128)(2,1)}, u32[]{:S(2)}) copy-start(bf16[2,256,256]{2,1,0:T(8,128)(2,1)} %constant.25.clone.zout) | copy-start | bytes 786436
  62.4 1.0 %copy-start = (f32[8,32,384]{2,1,0:T(8,128)S(1)}, f32[8,32,384]{2,1,0:T(8,128)}, u32[]{:S(2)}) copy-start(f32[8,32,384]{2,1,0:T(8,128)} %shard_map.154.back) | copy-start | bytes 1179652

commit v4 on v3

--- a/solution.py
+++ b/solution.py
@@ -73,7 +73,12 @@
     xin = wave_table(np.arange(NX), gx, NX, 1.0)
     xout = wave_table(gx, np.arange(NX), NX, -1.0)
     dx, hx = derivative_matrix(NX), cas_matrix(NX)
-    xmid = np.concatenate([dx.reshape(8, 8, NX), hx.reshape(8, 8, NX)], axis=1)
+    bands = np.stack([dx.reshape(8, 8, 8, 8), hx.reshape(8, 8, 8, 8)], axis=1)
+    xmid = []
+    for band in range(8):
+        ring = bands[[band, band ^ 1]][:, :, :, band % 2 :: 2]
+        xmid.append(ring.reshape(32, 32))
+    xmid = np.stack(xmid)
     dz = derivative_matrix(NZ)[:, 0]
     dz = np.concatenate([dz, dz, dz]).astype(np.float32)
     g_sq = squared_freq(NZ)[:, None, None] + squared_freq(NX)[None, :, None] + squared_freq(NY)[None, None, :]
@@ -159,7 +164,7 @@
     return jnp.concatenate([rows[z * count : z * count + count] for z in range(8)], axis=1)
 
 
-STEPS = ((2, 1), (1, 1), (3, 1), (2, 0), (0, 1), (1, 0), (3, 0))
+STEPS = ((2, 1), (1, 1), (3, 1), (0, 1), (2, 0), (1, 0), (3, 0))
 
 
 def partner(place, ring, pair):
@@ -179,7 +184,7 @@
     along, away, back, near_by,
     held, sticks, grid, psi, partial, summed, given,
     block, flux_x, flux_z, rho_hat, near_own, far_own, to_twin, from_twin,
-    by_x, by_x2, by_z, by_z2, by_z3, kernel_z, near, far, pot, pot_twin, picked,
+    crossed, by_x, by_x2, by_z, by_z2, by_z3, kernel_z, near, far, pot, pot_twin, picked,
     kernel_sem, load_sem, send, recv,
 ):
     s, p = lax.axis_index("state"), lax.axis_index("plane")
@@ -265,37 +270,52 @@
         place(partner(p, 4 - ring, pair), False)
 
     yin, xin, core, xmid = loaded("yin", "xin", "core", "xmid")
-    def waves(part):
+    def waves(part, quarter):
         lines = []
         for odd in range(2):
             rows = [
-                grid[pl.ds(pl.multiple_of(c * 512 + part * 256, 256), 256), odd * 128 : odd * 128 + 128] for c in range(2)
+                grid[
+                    pl.ds(pl.multiple_of(c * 512 + part * 256 + quarter * 128, 128), 128),
+                    odd * 128 : odd * 128 + 128,
+                ]
+                for c in range(2)
             ]
             turned = table_last(jnp.concatenate(rows, axis=1), yin)
             lines.append(
                 [
                     jnp.concatenate(
-                        [turned[z * 32 : z * 32 + 32, c * 128 : c * 128 + 128] for z in range(8)], axis=1
+                        [turned[z * 32 : z * 32 + 32, c * 128 : c * 128 + 128] for z in range(4)], axis=1
                     )
                     for c in range(2)
                 ]
             )
         lines = jnp.concatenate([lines[odd][c] for c in range(2) for odd in range(2)], axis=0)
         wave = four_first(xin, lines)
-        psi[:, lanes_of(part)] = wave
+        psi[:, pl.ds(pl.multiple_of(part * 1024 + quarter * 512, 512), 512)] = wave
         return (wave[:64] * wave[:64] + wave[64:] * wave[64:]) * (1.0 / STATES)
 
-    to_twin[...] = waves(twin)
-    copy = post(to_twin, from_twin, on_twin)
-    own = waves(half)
-    copy.wait()
-    summed[...] = own + from_twin[...]
-
-    copies = [post(summed.at[rows_of(partner(band, *step)), :], given.at[band], on_band(*step)) for step in STEPS]
+    cuts = [slice(0, 512), slice(512, 1024)]
+    swaps = []
+    for quarter, cut in enumerate(cuts):
+        to_twin[:, cut] = waves(twin, quarter)
+        swaps.append(post(to_twin.at[:, cut], from_twin.at[:, cut], on_twin))
+
+    copies = []
+    for quarter, cut in enumerate(cuts):
+        own = waves(half, quarter)
+        swaps[quarter].wait()
+        summed[:, cut] = own + from_twin[:, cut]
+        copies.append(
+            [
+                post(summed.at[rows_of(partner(band, *step)), cut], given.at[band, :, cut], on_band(*step))
+                for step in STEPS
+            ]
+        )
     rho = jnp.concatenate([core[half * 8 + z, rows_of(band), :] for z in range(8)], axis=1)
     rho = rho + summed[rows_of(band), :]
-    for copy, (ring, pair) in reversed(list(zip(copies, STEPS))):
-        copy.wait()
+    for first, second, (ring, pair) in reversed(list(zip(*copies, STEPS))):
+        first.wait()
+        second.wait()
         rho = rho + given[partner(band, 4 - ring, pair)]
     block[...] = rho
 
@@ -339,19 +359,31 @@
     def slope(at):
         return dz[at]
 
-    def mixed_x(source):
+    def all_ring(src, dst):
+        return [post(src, dst.at[rows_of(band // 2), :], on_band(*step)) for step in STEPS if step[1] == 0]
+
+    def mix_x(source, slot, count):
         high, low = parts(source[...])
-        return dot(xmid[0, band], high) + dot(xmid[0, band], low) + dot(xmid[1, band], high)
+        both = dot(xmid[0, band], high) + dot(xmid[0, band], low) + dot(xmid[1, band], high)
+        crossed[slot, 0, :count] = both[16 : 16 + count]
+        copy = post(crossed.at[slot, 0, :count], crossed.at[slot, 1, :count], on_band(0, 1))
+
+        def result():
+            copy.wait()
+            return both[:count] + crossed[slot, 1, :count]
+
+        return result
 
     dz, dy, hy, hx, xout, yout = loaded("dz", "dy", "hy", "hx", "xout", "yout")
-    by_x[rows_of(band), :] = rho
+    by_x[rows_of(band // 2), :] = rho
     by_z[p] = rho
-    z_copies, x_copies = all_planes(block, by_z), all_bands(block, by_x)
+    x_copies, z_copies = all_ring(block, by_x), all_planes(block, by_z)
     grad_z = Along(z_copies, by_z, slope, 0)
     grad_y = untile(table_last(tiles(rho, 8), dy), 8)
+    done(x_copies)
+    both = mix_x(by_x, 0, 16)
     grad_z.take(3)
-    done(x_copies)
-    both = mixed_x(by_x)
+    both = both()
     grad_x = both[:8]
     rho_xy = untile(table_last(tiles(both[8:], 8), hy), 8)
     rho_hat[...] = rho_xy
@@ -368,26 +400,26 @@
     grad_z = grad_z.result()
 
     v_local, twice = xc_terms(rho, grad_z * grad_z + grad_x * grad_x + grad_y * grad_y)
+    flux = twice * grad_x
+    flux_x[...] = flux
+    x_copies = all_ring(flux_x, by_x2)
+    by_x2[rows_of(band // 2), :] = flux
     flux = twice * grad_z
     flux_z[...] = flux
     z_copies = all_planes(flux_z, by_z2)
     by_z2[p] = flux
-    flux = twice * grad_x
-    flux_x[...] = flux
-    x_copies = all_bands(flux_x, by_x2)
-    by_x2[rows_of(band), :] = flux
     total = v_local - untile(table_last(tiles(twice * grad_y, 8), dy), 8)
 
     slant = Along(z_copies, by_z2, slope, 2)
     spread.swap()
-    slant.take(3)
+    done(x_copies)
+    slope_x = mix_x(by_x2, 1, 8)
     spread = spread.result()
     far_own[...] = spread
     f_copies = all_bands(far_own, far)
     far[rows_of(band), :] = spread
     slant.swap()
-    done(x_copies)
-    total = total - mixed_x(by_x2)[:8]
+    total = total - slope_x()
     total = total - slant.result()
     near_own[...] = total
     n_copies = all_bands(near_own, near)
@@ -416,29 +448,45 @@
                 at = pl.ds(pl.multiple_of(c * 512 + part * 256, 256), 256)
                 grid[at, odd * 128 : odd * 128 + 128] = turned[:, c * 128 : c * 128 + 128]
 
-    forces(pot[...], half)
-    copy.wait()
-    forces(pot_twin[...], twin)
-
-    high, low = parts(grid[...])
-    left = jnp.concatenate([high, low], axis=1)
-    copies = []
     order = STEPS + ((0, 0),)
-    for first in range(0, PLANES, 2):
-        steps = order[first : first + 2]
+
+    def places_of(steps):
         owners = [partner(p, *step) for step in steps]
         col = jnp.concatenate([columns_of(cols, owner) for owner in owners], axis=1)
         above = one_hot(col >> 8, 32)[None]
         below = one_hot(col & 255, 256).astype(BF16)
-        below = jnp.concatenate([below, below], axis=0)
-        found = [
-            jnp.sum(dot(left[rows : rows + 512], below).reshape(16, 32, 2 * CHUNK) * above, axis=1)
-            for rows in (0, 512)
-        ]
-        found = jnp.concatenate(found, axis=0)
-        for at, (step, owner) in enumerate(zip(steps, owners)):
-            chunk = found[:, at * CHUNK : (at + 1) * CHUNK]
-            picked[owner] = chunk
+        return owners, above, jnp.concatenate([below, below], axis=0)
+
+    def pick(at, above, below):
+        rows = grid[at, :]
+        found = dot(jnp.concatenate(parts(rows), axis=1), below)
+        return jnp.sum(found.reshape(-1, 32, 2 * CHUNK) * above, axis=1)
+
+    def pick_half(owners, above, below, part):
+        for c in range(2):
+            found = pick(pl.ds(pl.multiple_of(c * 512 + part * 256, 256), 256), above, below)
+            for at, owner in enumerate(owners):
+                picked[owner, pl.ds(pl.multiple_of(c * 16 + part * 8, 8), 8), :] = found[
+                    :, at * CHUNK : (at + 1) * CHUNK
+                ]
+
+    forces(pot[...], half)
+    ahead = places_of(order[:2])
+    pick_half(*ahead, half)
+    copy.wait()
+    forces(pot_twin[...], twin)
+    pick_half(*ahead, twin)
+    copies = [
+        post(picked.at[owner], back.at[p], on_plane(*step)) for step, owner in zip(order[:2], ahead[0])
+    ]
+    for first in range(2, PLANES, 2):
+        steps = order[first : first + 2]
+        owners, above, below = places_of(steps)
+        for c in range(2):
+            found = pick(slice(c * 512, c * 512 + 512), above, below)
+            for at, owner in enumerate(owners):
+                picked[owner, c * 16 : c * 16 + 16, :] = found[:, at * CHUNK : (at + 1) * CHUNK]
+        for step, owner in zip(steps, owners):
             if step == (0, 0):
                 fetch = pltpu.make_async_copy(picked.at[p], back.at[p], kernel_sem)
                 fetch.start()
@@ -453,7 +501,7 @@
     out[...] = force * mask[...].astype(F32)[None]
 
 
-COPIES = 7 * 10 + 5
+COPIES = 7 * 9 + 2 * 3 + 4 + 4
 
 
 def call(kernel, outs, ins, in_specs, out_specs, scratch=(), collective=None, limit=60):
@@ -477,7 +525,7 @@
     bundle, own, all_x, all_z = (PLANES, 32, CHUNK), (8, 1024), (64, 1024), (PLANES, 8, 1024)
     shapes = [bundle, bundle, (1024, 256), (128, 2048), (3, 2, 8, 1024), all_x, all_z]
     shapes += [own] * 6 + [all_x] * 2
-    shapes += [all_x] * 2 + [all_z] * 3 + [(65, 8, 128)] + [all_x] * 4 + [bundle]
+    shapes += [(2, 2, 16, 1024)] + [(32, 1024)] * 2 + [all_z] * 3 + [(65, 8, 128)] + [all_x] * 4 + [bundle]
     anywhere, whole = pl.BlockSpec(memory_space=pl.ANY), pl.BlockSpec(memory_space=pltpu.VMEM)
     back, = call(
         step_kernel,

time: 64.7 us -> 63.2 us (0.977)
  Pallas kernels: 63.5 us -> 62 us
    pallas_call x2, Pallas kernels: 63.5 us -> 62 us  [call(): pl.pallas_call(kernel, out_shape=[jax.ShapeDtypeStruct(shape, F32) for sh...]
where the time goes in v4:
time: 63.2 us; the launch traced here: 63 us
  Pallas kernels  62 us (98%)
  local copies, waits for them, and re-layouts  1 us (2%)
    pallas_call x2, Pallas kernels, call(): pl.pallas_call(kernel, out_shape=[jax.ShapeDtypeStruct(shape, F32) for sh...  62 us

profile of v4, /device:TPU:1, one launch (start us, length us, event | category | flops | bytes accessed | tf_op | source)
XLA Modules:
  0.0 63.0 jit_solution(216356273867845033)
XLA Ops:
  0.0 0.0 copy-start.1
  0.0 0.0 copy-start.2
  0.0 60.8 %shard_map.154.back = f32[8,32,384]{2,1,0:T(8,128)} custom-call(f32[8,65,8,128]{3,2,1,0:T(8,128)} %constant.35.clone.along, f32[2,128,384]{2,1,0:T(8,128)} %bitcast.5, s32[128,384]{1,0:T(8,128)} %mask.1, bf16[2,256,256]{2,1,0:T(8,128)(2,1)} %constant.24.clone.refs_2_, s32[1,3072]{1,0:T(1,128)} %bitcast.6, f32[384]{0:T(512)} %constant.34.clone.refs_4_, ...), custom_call_target="tpu_custom_call" | custom-call | tf_op jit(solution)/shard_map/pallas_call | solution.py:508
  60.8 0.0 copy-done.1
  60.9 0.0 copy-done.2
  60.9 0.0 copy-start
  60.9 1.0 %copy-done = f32[8,32,384]{2,1,0:T(8,128)S(1)} copy-done((f32[8,32,384]{2,1,0:T(8,128)S(1)}, f32[8,32,384]{2,1,0:T(8,128)}, u32[]{:S(2)}) %copy-start) | copy-done | bytes 393240
  61.9 1.1 %shard_map.155 = f32[2,128,384]{2,1,0:T(8,128)} custom-call(f32[8,32,384]{2,1,0:T(8,128)S(1)} %copy-done, s32[128,384]{1,0:T(8,128)S(1)} %copy-done.1, bf16[2,256,256]{2,1,0:T(8,128)(2,1)S(1)} %copy-done.2), custom_call_target="tpu_custom_call" | custom-call | tf_op jit(solution)/shard_map/pallas_call | solution.py:508
Async XLA Ops:
  0.0 60.9 %copy-start.1 = (s32[128,384]{1,0:T(8,128)S(1)}, s32[128,384]{1,0:T(8,128)}, u32[]{:S(2)}) copy-start(s32[128,384]{1,0:T(8,128)} %mask.1) | copy-start | bytes 589828
  0.0 60.9 %copy-start.2 = (bf16[2,256,256]{2,1,0:T(8,128)(2,1)S(1)}, bf16[2,256,256]{2,1,0:T(8,128)(2,1)}, u32[]{:S(2)}) copy-start(bf16[2,256,256]{2,1,0:T(8,128)(2,1)} %constant.25.clone.zout) | copy-start | bytes 786436
  60.9 1.0 %copy-start = (f32[8,32,384]{2,1,0:T(8,128)S(1)}, f32[8,32,384]{2,1,0:T(8,128)}, u32[]{:S(2)}) copy-start(f32[8,32,384]{2,1,0:T(8,128)} %shard_map.154.back) | copy-start | bytes 1179652

commit v5 on v4

--- a/solution.py
+++ b/solution.py
@@ -23,6 +23,9 @@
 F32 = jnp.float32
 BF16 = jnp.bfloat16
 MESH = pl.DeviceIdType.MESH
+
+
+STEPS = ((2, 1), (1, 1), (3, 1), (0, 1), (2, 0), (1, 0), (3, 0))
 
 
 def two_parts(table):
@@ -76,7 +79,8 @@
     bands = np.stack([dx.reshape(8, 8, 8, 8), hx.reshape(8, 8, 8, 8)], axis=1)
     xmid = []
     for band in range(8):
-        ring = bands[[band, band ^ 1]][:, :, :, band % 2 :: 2]
+        ring = [(band // 2 - step) % 4 * 2 + band % 2 for step in [0] + [ring for ring, pair in STEPS if pair == 0]]
+        ring = bands[[band, band ^ 1]][:, :, :, ring]
         xmid.append(ring.reshape(32, 32))
     xmid = np.stack(xmid)
     dz = derivative_matrix(NZ)[:, 0]
@@ -164,9 +168,6 @@
     return jnp.concatenate([rows[z * count : z * count + count] for z in range(8)], axis=1)
 
 
-STEPS = ((2, 1), (1, 1), (3, 1), (0, 1), (2, 0), (1, 0), (3, 0))
-
-
 def partner(place, ring, pair):
     return lax.rem(place // 2 + ring, 4) * 2 + lax.rem(place + pair, 2)
 
@@ -205,29 +206,53 @@
 
     loads = {}
     for at, name in enumerate(LOADED):
-        loads[name] = pltpu.make_async_copy(away[at], near_by[at], load_sem.at[at])
+        if name in FIRST:
+            size = away[at].shape[0] // 2
+            cuts = [pl.ds(side * size, size) for side in range(2)]
+            loads[name] = [
+                pltpu.make_async_copy(away[at].at[cut], near_by[at].at[cut], load_sem.at[side, at])
+                for side, cut in enumerate(cuts)
+            ]
+        else:
+            loads[name] = [pltpu.make_async_copy(away[at], near_by[at], load_sem.at[0, at])]
     for name in FIRST:
-        loads[name].start()
+        for copy in loads[name]:
+            copy.start()
 
     def loaded(*names):
         for name in names:
-            loads[name].wait()
+            for copy in loads[name]:
+                copy.wait()
         return [near_by[LOADED.index(name)] for name in names]
 
-    count = [0]
-
-    def post(src, dst, to):
-        at = count[0]
-        count[0] += 1
-        copy = pltpu.make_async_remote_copy(
-            src_ref=src, dst_ref=dst, send_sem=send.at[at], recv_sem=recv.at[at], device_id=to, device_id_type=MESH
-        )
-        copy.start()
-        return copy
-
-    def done(copies):
-        for copy in copies:
-            copy.wait()
+    sent, received = [], [0]
+
+    class Exchange:
+        def __init__(self, copies, span, each=False):
+            self.span, self.each, self.first = span, each, received[0]
+            received[0] += len(copies) if each else 1
+            self.copies = []
+            for at, (src, dst, to) in enumerate(copies):
+                copy = pltpu.make_async_remote_copy(
+                    src_ref=src,
+                    dst_ref=dst,
+                    send_sem=send.at[len(sent)],
+                    recv_sem=recv.at[self.first + at * each],
+                    device_id=to,
+                    device_id_type=MESH,
+                )
+                copy.start()
+                self.copies.append(copy)
+            sent.append(span)
+
+        def wait(self, at=None):
+            if at is None:
+                pltpu.make_async_copy(self.span, self.span, recv.at[self.first]).wait()
+            else:
+                self.copies[at].wait_recv()
+
+    def swap(src, dst, to):
+        return Exchange([(src, dst, to)], dst)
 
     def rows_of(other):
         return pl.ds(pl.multiple_of(other * 8, 8), 8)
@@ -237,22 +262,23 @@
 
     coeffs, mask, zin = loaded("coeffs", "mask", "zin")
     for name in LOADED[len(FIRST) :]:
-        loads[name].start()
+        loads[name][0].start()
     fetch = pltpu.make_async_copy(along.at[band], kernel_z, kernel_sem)
     fetch.start()
     values = (coeffs[...] * mask[...].astype(F32)[None]).reshape(2 * NZ, CHUNK)
     held[...] = table_first(zin, values).reshape(PLANES, 32, CHUNK)
     pl.semaphore_wait(barrier, 15)
-    copies = [post(held.at[partner(p, *step)], sticks.at[p], on_plane(*step)) for step in STEPS]
-    sticks[p] = held[p]
+    arrivals = Exchange(
+        [(held.at[partner(p, *step)], sticks.at[at], on_plane(*step)) for at, step in enumerate(STEPS)], sticks, True
+    )
 
     cols, = loaded("cols")
 
-    def place(chunk, fresh):
+    def place(values, chunk, fresh):
         col = columns_of(cols, chunk)
         above = one_hot(col >> 8, 32).astype(BF16)[None]
         below = one_hot(col & 255, 256).astype(BF16)
-        high, low = parts(sticks[chunk])
+        high, low = parts(values)
         below = jnp.concatenate([below, below], axis=1)
         for first in (0, 16):
             left = jnp.concatenate(
@@ -264,10 +290,10 @@
             else:
                 grid[rows] += dot_t(left, below)
 
-    place(p, True)
-    for copy, (ring, pair) in reversed(list(zip(copies, STEPS))):
-        copy.wait()
-        place(partner(p, 4 - ring, pair), False)
+    place(held[p], p, True)
+    for at, (ring, pair) in reversed(list(enumerate(STEPS))):
+        arrivals.wait(at)
+        place(sticks[at], partner(p, 4 - ring, pair), False)
 
     yin, xin, core, xmid = loaded("yin", "xin", "core", "xmid")
     def waves(part, quarter):
@@ -298,42 +324,46 @@
     swaps = []
     for quarter, cut in enumerate(cuts):
         to_twin[:, cut] = waves(twin, quarter)
-        swaps.append(post(to_twin.at[:, cut], from_twin.at[:, cut], on_twin))
-
-    copies = []
+        swaps.append(swap(to_twin.at[:, cut], from_twin.at[:, cut], on_twin))
+
+    sums = []
     for quarter, cut in enumerate(cuts):
         own = waves(half, quarter)
         swaps[quarter].wait()
         summed[:, cut] = own + from_twin[:, cut]
-        copies.append(
-            [
-                post(summed.at[rows_of(partner(band, *step)), cut], given.at[band, :, cut], on_band(*step))
-                for step in STEPS
-            ]
+        sums.append(
+            Exchange(
+                [
+                    (summed.at[rows_of(partner(band, *step)), cut], given.at[at, :, cut], on_band(*step))
+                    for at, step in enumerate(STEPS)
+                ],
+                given.at[:, :, cut],
+            )
         )
     rho = jnp.concatenate([core[half * 8 + z, rows_of(band), :] for z in range(8)], axis=1)
     rho = rho + summed[rows_of(band), :]
-    for first, second, (ring, pair) in reversed(list(zip(*copies, STEPS))):
-        first.wait()
-        second.wait()
-        rho = rho + given[partner(band, 4 - ring, pair)]
+    for part in sums:
+        part.wait()
+    for at in range(len(STEPS)):
+        rho = rho + given[at]
     block[...] = rho
 
     def all_bands(src, dst):
-        return [post(src, dst.at[rows_of(band), :], on_band(*step)) for step in STEPS]
+        copies = [(src, dst.at[rows_of(band), :], on_band(*step)) for step in STEPS]
+        return Exchange(copies, dst.at[pl.ds(0, 56), :])
 
     def all_planes(src, dst):
-        return [post(src, dst.at[p], on_plane(*step)) for step in STEPS]
+        return Exchange([(src, dst.at[at], on_plane(*step)) for at, step in enumerate(STEPS)], dst, True)
 
     class Along:
-        def __init__(self, copies, source, weight, slot):
-            self.arrivals = list(reversed(list(zip(copies, STEPS))))
-            self.source, self.weight, self.slot = source, weight, slot
+        def __init__(self, own, arrivals, source, weight, slot):
+            self.arrivals, self.source, self.weight, self.slot = arrivals, source, weight, slot
+            self.left = list(reversed(range(len(STEPS))))
             self.sums = [[jnp.zeros((8, 128), F32)] * 8 for _ in range(2)]
-            self.add(p)
-
-        def add(self, other):
-            held = [self.source[other, :, z * 128 : z * 128 + 128] for z in range(8)]
+            self.add(own, p)
+
+        def add(self, planes, other):
+            held = [planes[:, z * 128 : z * 128 + 128] for z in range(8)]
             for sums, part in zip(self.sums, (half, twin)):
                 start = (p - other) * 16 + (part - half) * 8 + 128
                 factors = {shift: self.weight(start + shift) for shift in range(-7, 8)}
@@ -342,15 +372,16 @@
                         sums[to] = sums[to] + factors[to - z] * held[z]
 
         def take(self, number):
-            for copy, (ring, pair) in self.arrivals[:number]:
-                copy.wait()
-                self.add(partner(p, 4 - ring, pair))
-            self.arrivals = self.arrivals[number:]
+            for at in self.left[:number]:
+                ring, pair = STEPS[at]
+                self.arrivals.wait(at)
+                self.add(self.source[at], partner(p, 4 - ring, pair))
+            self.left = self.left[number:]
 
         def swap(self):
-            self.take(len(self.arrivals))
+            self.take(len(self.left))
             partial[self.slot, 0] = jnp.concatenate(self.sums[1], axis=1)
-            self.copy = post(partial.at[self.slot, 0], partial.at[self.slot, 1], on_twin)
+            self.copy = swap(partial.at[self.slot, 0], partial.at[self.slot, 1], on_twin)
 
         def result(self):
             self.copy.wait()
@@ -360,13 +391,15 @@
         return dz[at]
 
     def all_ring(src, dst):
-        return [post(src, dst.at[rows_of(band // 2), :], on_band(*step)) for step in STEPS if step[1] == 0]
-
-    def mix_x(source, slot, count):
-        high, low = parts(source[...])
+        steps = [step for step in STEPS if step[1] == 0]
+        copies = [(src, dst.at[at], on_band(*step)) for at, step in enumerate(steps)]
+        return Exchange(copies, dst)
+
+    def mix_x(own, source, slot, count):
+        high, low = parts(jnp.concatenate([own] + [source[at] for at in range(3)], axis=0))
         both = dot(xmid[0, band], high) + dot(xmid[0, band], low) + dot(xmid[1, band], high)
         crossed[slot, 0, :count] = both[16 : 16 + count]
-        copy = post(crossed.at[slot, 0, :count], crossed.at[slot, 1, :count], on_band(0, 1))
+        copy = swap(crossed.at[slot, 0, :count], crossed.at[slot, 1, :count], on_band(0, 1))
 
         def result():
             copy.wait()
@@ -375,20 +408,17 @@
         return result
 
     dz, dy, hy, hx, xout, yout = loaded("dz", "dy", "hy", "hx", "xout", "yout")
-    by_x[rows_of(band // 2), :] = rho
-    by_z[p] = rho
-    x_copies, z_copies = all_ring(block, by_x), all_planes(block, by_z)
-    grad_z = Along(z_copies, by_z, slope, 0)
+    ring, planes = all_ring(block, by_x), all_planes(block, by_z)
+    grad_z = Along(rho, planes, by_z, slope, 0)
     grad_y = untile(table_last(tiles(rho, 8), dy), 8)
-    done(x_copies)
-    both = mix_x(by_x, 0, 16)
+    ring.wait()
+    both = mix_x(rho, by_x, 0, 16)
     grad_z.take(3)
     both = both()
     grad_x = both[:8]
     rho_xy = untile(table_last(tiles(both[8:], 8), hy), 8)
     rho_hat[...] = rho_xy
-    r_copies = all_planes(rho_hat, by_z3)
-    by_z3[p] = rho_xy
+    planes = all_planes(rho_hat, by_z3)
     grad_z.swap()
     fetch.wait()
 
@@ -396,40 +426,37 @@
         at = lax.rem(at, 128)
         return kernel_z[jnp.minimum(at, 128 - at)]
 
-    spread = Along(r_copies, by_z3, even, 1)
+    spread = Along(rho_xy, planes, by_z3, even, 1)
     grad_z = grad_z.result()
 
     v_local, twice = xc_terms(rho, grad_z * grad_z + grad_x * grad_x + grad_y * grad_y)
-    flux = twice * grad_x
-    flux_x[...] = flux
-    x_copies = all_ring(flux_x, by_x2)
-    by_x2[rows_of(band // 2), :] = flux
-    flux = twice * grad_z
-    flux_z[...] = flux
-    z_copies = all_planes(flux_z, by_z2)
-    by_z2[p] = flux
+    along_x, across = twice * grad_x, twice * grad_z
+    flux_x[...] = along_x
+    ring = all_ring(flux_x, by_x2)
+    flux_z[...] = across
+    planes = all_planes(flux_z, by_z2)
     total = v_local - untile(table_last(tiles(twice * grad_y, 8), dy), 8)
 
-    slant = Along(z_copies, by_z2, slope, 2)
+    slant = Along(across, planes, by_z2, slope, 2)
     spread.swap()
-    done(x_copies)
-    slope_x = mix_x(by_x2, 1, 8)
+    ring.wait()
+    slope_x = mix_x(along_x, by_x2, 1, 8)
     spread = spread.result()
     far_own[...] = spread
-    f_copies = all_bands(far_own, far)
+    fars = all_bands(far_own, far)
     far[rows_of(band), :] = spread
     slant.swap()
     total = total - slope_x()
     total = total - slant.result()
     near_own[...] = total
-    n_copies = all_bands(near_own, near)
+    nears = all_bands(near_own, near)
     near[rows_of(band), :] = total
 
-    done(f_copies)
+    fars.wait()
     turned = untile(table_last(tiles(four_first(hx, far[...]), 64), hy), 64)
-    done(n_copies)
+    nears.wait()
     pot[...] = near[...] + turned
-    copy = post(pot, pot_twin, on_twin)
+    copy = swap(pot, pot_twin, on_twin)
 
     def forces(potential, part):
         lanes = lanes_of(part)
@@ -476,9 +503,26 @@
     copy.wait()
     forces(pot_twin[...], twin)
     pick_half(*ahead, twin)
-    copies = [
-        post(picked.at[owner], back.at[p], on_plane(*step)) for step, owner in zip(order[:2], ahead[0])
-    ]
+    arrived = received[0]
+    returns = []
+
+    def give(step, owner):
+        if step == (0, 0):
+            copy = pltpu.make_async_copy(picked.at[p], back.at[p], kernel_sem)
+        else:
+            copy = pltpu.make_async_remote_copy(
+                src_ref=picked.at[owner],
+                dst_ref=back.at[p],
+                send_sem=send.at[len(sent)],
+                recv_sem=recv.at[arrived],
+                device_id=on_plane(*step),
+                device_id_type=MESH,
+            )
+        copy.start()
+        returns.append(copy)
+
+    for step, owner in zip(order[:2], ahead[0]):
+        give(step, owner)
     for first in range(2, PLANES, 2):
         steps = order[first : first + 2]
         owners, above, below = places_of(steps)
@@ -487,13 +531,12 @@
             for at, owner in enumerate(owners):
                 picked[owner, c * 16 : c * 16 + 16, :] = found[:, at * CHUNK : (at + 1) * CHUNK]
         for step, owner in zip(steps, owners):
-            if step == (0, 0):
-                fetch = pltpu.make_async_copy(picked.at[p], back.at[p], kernel_sem)
-                fetch.start()
-                copies.append(fetch)
-            else:
-                copies.append(post(picked.at[owner], back.at[p], on_plane(*step)))
-    done(copies)
+            give(step, owner)
+    returns[-1].wait()
+    seven = back.at[pl.ds(0, 7)]
+    pltpu.make_async_copy(seven, seven, recv.at[arrived]).wait()
+    for at, span in enumerate(sent + [seven]):
+        pltpu.make_async_copy(span, span, send.at[at]).wait()
 
 
 def last_kernel(back, mask, zout, out):
@@ -501,7 +544,7 @@
     out[...] = force * mask[...].astype(F32)[None]
 
 
-COPIES = 7 * 9 + 2 * 3 + 4 + 4
+SENDS, ARRIVALS = 19, 43
 
 
 def call(kernel, outs, ins, in_specs, out_specs, scratch=(), collective=None, limit=60):
@@ -522,10 +565,10 @@
 def on_device(coeffs, mask, stick_cols, core):
     t = {name: jnp.asarray(table) for name, table in tables().items()}
     t.update(coeffs=coeffs.reshape(2, NZ, CHUNK), mask=mask, cols=stick_cols.reshape(1, NSTICK), core=core)
-    bundle, own, all_x, all_z = (PLANES, 32, CHUNK), (8, 1024), (64, 1024), (PLANES, 8, 1024)
-    shapes = [bundle, bundle, (1024, 256), (128, 2048), (3, 2, 8, 1024), all_x, all_z]
+    bundle, own, all_x, all_z = (PLANES, 32, CHUNK), (8, 1024), (64, 1024), (7, 8, 1024)
+    shapes = [bundle, (7, 32, CHUNK), (1024, 256), (128, 2048), (3, 2, 8, 1024), all_x, all_z]
     shapes += [own] * 6 + [all_x] * 2
-    shapes += [(2, 2, 16, 1024)] + [(32, 1024)] * 2 + [all_z] * 3 + [(65, 8, 128)] + [all_x] * 4 + [bundle]
+    shapes += [(2, 2, 16, 1024)] + [(3, 8, 1024)] * 2 + [all_z] * 3 + [(65, 8, 128)] + [all_x] * 4 + [bundle]
     anywhere, whole = pl.BlockSpec(memory_space=pl.ANY), pl.BlockSpec(memory_space=pltpu.VMEM)
     back, = call(
         step_kernel,
@@ -538,8 +581,8 @@
             for name in LOADED
         ]
         + [pltpu.VMEM(shape, F32) for shape in shapes]
-        + [pltpu.SemaphoreType.DMA, pltpu.SemaphoreType.DMA((len(LOADED),))]
-        + [pltpu.SemaphoreType.DMA((COPIES,)), pltpu.SemaphoreType.DMA((COPIES,))],
+        + [pltpu.SemaphoreType.DMA, pltpu.SemaphoreType.DMA((2, len(LOADED)))]
+        + [pltpu.SemaphoreType.DMA((SENDS,)), pltpu.SemaphoreType.DMA((ARRIVALS,))],
         collective=0,
     )
     forces, = call(

time: 63.2 us -> 61.8 us (0.978)
  Pallas kernels: 62 us -> 60.6 us
    pallas_call x2, Pallas kernels: 62 us -> 60.6 us  [call(): pl.pallas_call(kernel, out_shape=[jax.ShapeDtypeStruct(shape, F32) for sh...]
where the time goes in v5:
time: 61.8 us; the launch traced here: 61.7 us
  Pallas kernels  60.6 us (98%)
  local copies, waits for them, and re-layouts  1 us (2%)
    pallas_call x2, Pallas kernels, call(): pl.pallas_call(kernel, out_shape=[jax.ShapeDtypeStruct(shape, F32) for sh...  60.6 us

profile of v5, /device:TPU:1, one launch (start us, length us, event | category | flops | bytes accessed | tf_op | source)
XLA Modules:
  0.0 61.7 jit_solution(1414461610815074914)
XLA Ops:
  0.0 0.0 copy-start.1
  0.0 0.0 copy-start.2
  0.0 59.5 %shard_map.154.back = f32[8,32,384]{2,1,0:T(8,128)} custom-call(f32[8,65,8,128]{3,2,1,0:T(8,128)} %constant.35.clone.along, f32[2,128,384]{2,1,0:T(8,128)} %bitcast.5, s32[128,384]{1,0:T(8,128)} %mask.1, bf16[2,256,256]{2,1,0:T(8,128)(2,1)} %constant.24.clone.refs_2_, s32[1,3072]{1,0:T(1,128)} %bitcast.6, f32[384]{0:T(512)} %constant.34.clone.refs_4_, ...), custom_call_target="tpu_custom_call" | custom-call | tf_op jit(solution)/shard_map/pallas_call | solution.py:551
  59.5 0.0 copy-done.1
  59.5 0.0 copy-done.2
  59.5 0.0 copy-start
  59.5 1.0 %copy-done = f32[8,32,384]{2,1,0:T(8,128)S(1)} copy-done((f32[8,32,384]{2,1,0:T(8,128)S(1)}, f32[8,32,384]{2,1,0:T(8,128)}, u32[]{:S(2)}) %copy-start) | copy-done | bytes 393240
  60.5 1.1 %shard_map.155 = f32[2,128,384]{2,1,0:T(8,128)} custom-call(f32[8,32,384]{2,1,0:T(8,128)S(1)} %copy-done, s32[128,384]{1,0:T(8,128)S(1)} %copy-done.1, bf16[2,256,256]{2,1,0:T(8,128)(2,1)S(1)} %copy-done.2), custom_call_target="tpu_custom_call" | custom-call | tf_op jit(solution)/shard_map/pallas_call | solution.py:551
Async XLA Ops:
  0.0 59.5 %copy-start.1 = (s32[128,384]{1,0:T(8,128)S(1)}, s32[128,384]{1,0:T(8,128)}, u32[]{:S(2)}) copy-start(s32[128,384]{1,0:T(8,128)} %mask.1) | copy-start | bytes 589828
  0.0 59.5 %copy-start.2 = (bf16[2,256,256]{2,1,0:T(8,128)(2,1)S(1)}, bf16[2,256,256]{2,1,0:T(8,128)(2,1)}, u32[]{:S(2)}) copy-start(bf16[2,256,256]{2,1,0:T(8,128)(2,1)} %constant.25.clone.zout) | copy-start | bytes 786436
  59.5 1.0 %copy-start = (f32[8,32,384]{2,1,0:T(8,128)S(1)}, f32[8,32,384]{2,1,0:T(8,128)}, u32[]{:S(2)}) copy-start(f32[8,32,384]{2,1,0:T(8,128)} %shard_map.154.back) | copy-start | bytes 1179652

commit v6 on v5

--- a/solution.py
+++ b/solution.py
@@ -139,10 +139,6 @@
     return jnp.where(places == values, 1.0, 0.0)
 
 
-def columns_of(cols, chunk):
-    return cols[:, pl.ds(pl.multiple_of(chunk * CHUNK, 128), CHUNK)]
-
-
 def xc_terms(rho, g):
     kappa, mu = 0.804, 0.2195
     exch = 0.75 * (3.0 / math.pi) ** (1.0 / 3.0)
@@ -183,7 +179,7 @@
 
 def work(
     along, away, back, near_by,
-    held, sticks, grid, psi, partial, summed, given,
+    aboves, belows, held, sticks, grid, psi, partial, summed, given,
     block, flux_x, flux_z, rho_hat, near_own, far_own, to_twin, from_twin,
     crossed, by_x, by_x2, by_z, by_z2, by_z3, kernel_z, near, far, pot, pot_twin, picked,
     kernel_sem, load_sem, send, recv,
@@ -206,23 +202,13 @@
 
     loads = {}
     for at, name in enumerate(LOADED):
-        if name in FIRST:
-            size = away[at].shape[0] // 2
-            cuts = [pl.ds(side * size, size) for side in range(2)]
-            loads[name] = [
-                pltpu.make_async_copy(away[at].at[cut], near_by[at].at[cut], load_sem.at[side, at])
-                for side, cut in enumerate(cuts)
-            ]
-        else:
-            loads[name] = [pltpu.make_async_copy(away[at], near_by[at], load_sem.at[0, at])]
+        loads[name] = pltpu.make_async_copy(away[at], near_by[at], load_sem.at[at])
     for name in FIRST:
-        for copy in loads[name]:
-            copy.start()
+        loads[name].start()
 
     def loaded(*names):
         for name in names:
-            for copy in loads[name]:
-                copy.wait()
+            loads[name].wait()
         return [near_by[LOADED.index(name)] for name in names]
 
     sent, received = [], [0]
@@ -262,7 +248,7 @@
 
     coeffs, mask, zin = loaded("coeffs", "mask", "zin")
     for name in LOADED[len(FIRST) :]:
-        loads[name][0].start()
+        loads[name].start()
     fetch = pltpu.make_async_copy(along.at[band], kernel_z, kernel_sem)
     fetch.start()
     values = (coeffs[...] * mask[...].astype(F32)[None]).reshape(2 * NZ, CHUNK)
@@ -274,10 +260,13 @@
 
     cols, = loaded("cols")
 
+    for chunk in range(PLANES):
+        col = cols[:, chunk * CHUNK : chunk * CHUNK + CHUNK]
+        aboves[chunk] = one_hot(col >> 8, 32).astype(BF16)
+        belows[chunk] = one_hot(col & 255, 256).astype(BF16)
+
     def place(values, chunk, fresh):
-        col = columns_of(cols, chunk)
-        above = one_hot(col >> 8, 32).astype(BF16)[None]
-        below = one_hot(col & 255, 256).astype(BF16)
+        above, below = aboves[chunk][None], belows[chunk]
         high, low = parts(values)
         below = jnp.concatenate([below, below], axis=1)
         for first in (0, 16):
@@ -353,12 +342,13 @@
         return Exchange(copies, dst.at[pl.ds(0, 56), :])
 
     def all_planes(src, dst):
-        return Exchange([(src, dst.at[at], on_plane(*step)) for at, step in enumerate(STEPS)], dst, True)
+        copies = [(src, dst.at[at], on_plane(*step)) for at, step in enumerate(STEPS)]
+        return [Exchange(copies[cut], dst.at[cut]) for cut in (slice(0, 4), slice(4, 7))]
 
     class Along:
         def __init__(self, own, arrivals, source, weight, slot):
             self.arrivals, self.source, self.weight, self.slot = arrivals, source, weight, slot
-            self.left = list(reversed(range(len(STEPS))))
+            self.left = [slice(0, 4), slice(4, 7)]
             self.sums = [[jnp.zeros((8, 128), F32)] * 8 for _ in range(2)]
             self.add(own, p)
 
@@ -371,15 +361,15 @@
                     for z in range(8):
                         sums[to] = sums[to] + factors[to - z] * held[z]
 
-        def take(self, number):
-            for at in self.left[:number]:
-                ring, pair = STEPS[at]
-                self.arrivals.wait(at)
+        def take(self):
+            cut = self.left.pop()
+            self.arrivals.pop().wait()
+            for at, (ring, pair) in reversed(list(enumerate(STEPS))[cut]):
                 self.add(self.source[at], partner(p, 4 - ring, pair))
-            self.left = self.left[number:]
 
         def swap(self):
-            self.take(len(self.left))
+            while self.left:
+                self.take()
             partial[self.slot, 0] = jnp.concatenate(self.sums[1], axis=1)
             self.copy = swap(partial.at[self.slot, 0], partial.at[self.slot, 1], on_twin)
 
@@ -413,7 +403,7 @@
     grad_y = untile(table_last(tiles(rho, 8), dy), 8)
     ring.wait()
     both = mix_x(rho, by_x, 0, 16)
-    grad_z.take(3)
+    grad_z.take()
     both = both()
     grad_x = both[:8]
     rho_xy = untile(table_last(tiles(both[8:], 8), hy), 8)
@@ -479,15 +469,14 @@
 
     def places_of(steps):
         owners = [partner(p, *step) for step in steps]
-        col = jnp.concatenate([columns_of(cols, owner) for owner in owners], axis=1)
-        above = one_hot(col >> 8, 32)[None]
-        below = one_hot(col & 255, 256).astype(BF16)
-        return owners, above, jnp.concatenate([below, below], axis=0)
+        above = jnp.concatenate([aboves[owner].astype(F32) for owner in owners], axis=1)
+        below = jnp.concatenate([belows[owner] for owner in owners], axis=1)
+        return owners, above[None], jnp.concatenate([below, below], axis=0)
 
     def pick(at, above, below):
         rows = grid[at, :]
         found = dot(jnp.concatenate(parts(rows), axis=1), below)
-        return jnp.sum(found.reshape(-1, 32, 2 * CHUNK) * above, axis=1)
+        return jnp.sum(found.reshape(-1, 32, found.shape[1]) * above, axis=1)
 
     def pick_half(owners, above, below, part):
         for c in range(2):
@@ -498,7 +487,7 @@
                 ]
 
     forces(pot[...], half)
-    ahead = places_of(order[:2])
+    ahead = places_of(order[:1])
     pick_half(*ahead, half)
     copy.wait()
     forces(pot_twin[...], twin)
@@ -521,9 +510,8 @@
         copy.start()
         returns.append(copy)
 
-    for step, owner in zip(order[:2], ahead[0]):
-        give(step, owner)
-    for first in range(2, PLANES, 2):
+    give(order[0], ahead[0][0])
+    for first in range(1, PLANES, 2):
         steps = order[first : first + 2]
         owners, above, below = places_of(steps)
         for c in range(2):
@@ -544,10 +532,10 @@
     out[...] = force * mask[...].astype(F32)[None]
 
 
-SENDS, ARRIVALS = 19, 43
-
-
-def call(kernel, outs, ins, in_specs, out_specs, scratch=(), collective=None, limit=60):
+SENDS, ARRIVALS = 22, 28
+
+
+def call(kernel, outs, ins, in_specs, out_specs, scratch=(), collective=None, kib=60 * 1024):
     return pl.pallas_call(
         kernel,
         out_shape=[jax.ShapeDtypeStruct(shape, F32) for shape in outs],
@@ -557,7 +545,7 @@
         compiler_params=pltpu.CompilerParams(
             collective_id=collective,
             has_side_effects=collective is not None,
-            vmem_limit_bytes=limit * 1024 * 1024,
+            vmem_limit_bytes=kib * 1024,
         ),
     )(*ins)
 
@@ -580,8 +568,9 @@
             (pltpu.SMEM if name == "dz" else pltpu.VMEM)(t[name].shape, t[name].dtype)
             for name in LOADED
         ]
+        + [pltpu.VMEM((PLANES, rows, CHUNK), BF16) for rows in (32, 256)]
         + [pltpu.VMEM(shape, F32) for shape in shapes]
-        + [pltpu.SemaphoreType.DMA, pltpu.SemaphoreType.DMA((2, len(LOADED)))]
+        + [pltpu.SemaphoreType.DMA, pltpu.SemaphoreType.DMA((len(LOADED),))]
         + [pltpu.SemaphoreType.DMA((SENDS,)), pltpu.SemaphoreType.DMA((ARRIVALS,))],
         collective=0,
     )
@@ -591,7 +580,7 @@
         [back, mask, t["zout"]],
         [whole] * 3,
         [whole],
-        limit=8,
+        kib=54600,
     )
     return forces.reshape(2, 1, NZ, CHUNK)
 

time: 61.8 us -> 61.8 us (level)
  Pallas kernels: 60.6 us -> 61.6 us
  local copies, waits for them, and re-layouts: 1 us -> 0.01 us
    pallas_call x2, Pallas kernels: 60.6 us -> 61.6 us  [call(): pl.pallas_call(kernel, out_shape=[jax.ShapeDtypeStruct(shape, F32) for sh...]
    unnamed x6 -> x4, local copies, waits for them, and re-layouts: 1 us -> 0.01 us
where the time goes in v6:
time: 61.8 us; the launch traced here: 61.7 us
  Pallas kernels  61.6 us (100%)
    pallas_call x2, Pallas kernels, call(): pl.pallas_call(kernel, out_shape=[jax.ShapeDtypeStruct(shape, F32) for sh...  61.6 us

profile of v6, /device:TPU:1, one launch (start us, length us, event | category | flops | bytes accessed | tf_op | source)
XLA Modules:
  0.0 61.7 jit_solution(9625544488879694215)
XLA Ops:
  0.0 0.0 copy-start
  0.0 0.0 copy-start.1
  0.0 59.5 %shard_map.154.back = f32[8,32,384]{2,1,0:T(8,128)} custom-call(f32[8,65,8,128]{3,2,1,0:T(8,128)} %constant.35.clone.along, f32[2,128,384]{2,1,0:T(8,128)} %bitcast.5, s32[128,384]{1,0:T(8,128)} %mask.1, bf16[2,256,256]{2,1,0:T(8,128)(2,1)} %constant.24.clone.refs_2_, s32[1,3072]{1,0:T(1,128)} %bitcast.6, f32[384]{0:T(512)} %constant.34.clone.refs_4_, ...), custom_call_target="tpu_custom_call" | custom-call | tf_op jit(solution)/shard_map/pallas_call | solution.py:539
  59.5 0.0 copy-done
  59.6 0.0 copy-done.1
  59.6 2.1 %shard_map.155 = f32[2,128,384]{2,1,0:T(8,128)} custom-call(f32[8,32,384]{2,1,0:T(8,128)} %shard_map.154.back, s32[128,384]{1,0:T(8,128)S(1)} %copy-done, bf16[2,256,256]{2,1,0:T(8,128)(2,1)S(1)} %copy-done.1), custom_call_target="tpu_custom_call" | custom-call | tf_op jit(solution)/shard_map/pallas_call | solution.py:539
Async XLA Ops:
  0.0 59.5 %copy-start = (s32[128,384]{1,0:T(8,128)S(1)}, s32[128,384]{1,0:T(8,128)}, u32[]{:S(2)}) copy-start(s32[128,384]{1,0:T(8,128)} %mask.1) | copy-start | bytes 589828
  0.0 59.6 %copy-start.1 = (bf16[2,256,256]{2,1,0:T(8,128)(2,1)S(1)}, bf16[2,256,256]{2,1,0:T(8,128)(2,1)}, u32[]{:S(2)}) copy-start(bf16[2,256,256]{2,1,0:T(8,128)(2,1)} %constant.25.clone.zout) | copy-start | bytes 786436
